TPU v7x, 32 devices: a whole 2x2x4 slice. The times are simulated.
32 devices in a mesh: pages: 16 (over z, x, core), tok: 2 (over y).
Axes of the slice: x: 2, y: 2, z: 4, core: 2. Of those that a mesh axis runs over, the one named last changes fastest.
Arguments:
- queries: bfloat16 [32, 32, 128], P('pages'), may hold values from -50 to 50
- pages: bfloat16 [16, 1024, 128], P('pages', 'tok'), may hold values from -10 to 10
- pad_counts: int32 [16], P('pages'), may hold values from 0 to 511
- labels: int32 [32, 16], P(None, 'pages'), may hold values 0 or 1
Outputs:
- query_grad: float32 [32, 32, 128], P('pages')
- page_grad: float32 [16, 1024, 128], P('pages', 'tok')
- page_loss: float32 [16], P('pages')
All inputs are finite; a program needn't handle non-finite values. No bound on the sum of `labels` on one device may be relied on, other than what follows from the above.
Results may differ from a plain program's by a relative error of at most 0.0025.
Values may be sent and summed in bfloat16 or wider, within the bound.
No kernel may reach another device: no remote copies, remote signals or barrier semaphores. Data moves between devices by JAX's collectives and lax.ppermute only.
A program may use at most 64 MiB of HBM per device.

v0:
```python
import math

import jax
import jax.numpy as jnp
from jax import lax
from jax.sharding import PartitionSpec as P

LP = 1024


MASKED = -1000000000.0
LOGIT_SPAN = 8.0
CENTRE_SHIFT = 0.5
FILL_SHARE = 0.75


def combined_all(value, axis, combine):
    everything = lax.all_gather(value, axis)
    first = everything[0]

    def lap(k, so_far):
        return combine(so_far, everything[k])

    return lax.fori_loop(1, lax.axis_size(axis), lap, first)


def combine_smooth(former, latter):
    highest = jnp.maximum(former, latter)
    return highest + jnp.log(jnp.exp(former - highest) + jnp.exp(latter - highest))


def on_device(queries, pages, pad_counts, labels):
    query_count, query_len, feature_width = queries.shape
    local_pages, local_tokens, _ = pages.shape
    score_scale = feature_width ** (-0.5)
    token_offset = lax.axis_index("tok") * local_tokens
    positions = token_offset + jnp.arange(local_tokens, dtype=jnp.int32)
    usable = positions[None, :] < (LP - pad_counts)[:, None]
    gathered = lax.all_gather(queries, "pages", axis=0, tiled=True)
    query_total = gathered.shape[0]
    row_count = query_total * query_len
    query_rows = gathered.reshape(row_count, feature_width)
    block_rows = math.gcd(row_count, 512)
    block_count = row_count // block_rows

    def scores_for(query_block, page_no):
        raw = (
            lax.dot_general(
                query_block,
                pages[page_no],
                (((1,), (1,)), ((), ())),
                preferred_element_type=jnp.float32,
            )
            * score_scale
        )
        return jnp.where(usable[page_no][None, :], raw, MASKED)

    def forward_block(block_index, running):
        offset = block_index * block_rows
        query_block = lax.dynamic_slice_in_dim(query_rows, offset, block_rows, 0)
        scores = scores_for(query_block, 0)
        highest = jnp.max(scores, axis=1)
        columns = [highest + jnp.log(jnp.sum(jnp.exp(scores - highest[:, None]), axis=1))]
        partial_value = jnp.stack(columns, axis=1)
        return lax.dynamic_update_slice_in_dim(running, partial_value, offset, 0)

    buffered = lax.fori_loop(
        0, block_count, forward_block, jnp.zeros((row_count, local_pages), jnp.float32)
    )
    smooth = combined_all(buffered, "tok", combine_smooth)
    similarity = smooth.reshape(query_total, query_len, local_pages).sum(axis=1)
    label_sign = 2.0 * labels.astype(jnp.float32) - 1.0
    logit_gain = LOGIT_SPAN / query_len
    centre = query_len * (CENTRE_SHIFT + math.log(FILL_SHARE * LP))
    logits = logit_gain * (similarity - centre)
    page_loss = jnp.sum(jax.nn.softplus(-label_sign * logits), axis=0)
    slope = logit_gain * (-label_sign * jax.nn.sigmoid(-label_sign * logits))
    row_slope = jnp.repeat(slope, query_len, axis=0)

    def backward_block(block_index, running):
        query_terms, page_terms = running
        offset = block_index * block_rows
        query_block = lax.dynamic_slice_in_dim(query_rows, offset, block_rows, 0)
        smooth_block = lax.dynamic_slice_in_dim(smooth, offset, block_rows, 0)
        slope_block = lax.dynamic_slice_in_dim(row_slope, offset, block_rows, 0)
        scores = scores_for(query_block, 0)
        weights = jnp.where(usable[0][None, :], jnp.exp(scores - smooth_block[:, 0][:, None]), 0.0)
        scaled = (weights * slope_block[:, 0][:, None]).astype(jnp.bfloat16)
        summed = jnp.dot(scaled, pages[0], preferred_element_type=jnp.float32)
        gradients = [
            lax.dot_general(
                scaled, query_block, (((0,), (0,)), ((), ())), preferred_element_type=jnp.float32
            )
        ]
        page_terms = page_terms + jnp.stack(gradients, axis=0)
        query_terms = lax.dynamic_update_slice_in_dim(query_terms, summed * score_scale, offset, 0)
        return (query_terms, page_terms)

    start_terms = (
        jnp.zeros((row_count, feature_width), jnp.float32),
        jnp.zeros((local_pages, local_tokens, feature_width), jnp.float32),
    )
    query_terms, page_terms = lax.fori_loop(0, block_count, backward_block, start_terms)
    page_grad = page_terms * score_scale
    owned = lax.psum_scatter(query_terms, "pages", scatter_dimension=0, tiled=True)
    owned = lax.psum(owned, "tok")
    query_grad = owned.reshape(query_count, query_len, feature_width)
    return (query_grad, page_grad, page_loss)


def solution(mesh):
    return jax.shard_map(
        on_device,
        mesh=mesh,
        in_specs=(P("pages", None, None), P("pages", "tok", None), P("pages"), P(None, "pages")),
        out_specs=(P("pages", None, None), P("pages", "tok", None), P("pages")),
        check_vma=False,
    )
```

profile of v0, /device:TPU:0, one launch (start us, length us, event | category | flops | bytes accessed | tf_op | source)
XLA Modules:
  0.0 112.6 jit_solution(9280587860546555923)
XLA Ops:
  7.2 0.0 reduce-scatter.2.cloned.1.call-start
  7.9 0.0 copy-start
  7.9 24.2 %all_gather.9 = bf16[32,32,128]{2,1,0:T(8,128)(2,1)S(1)} all-gather(bf16[2,32,128]{2,1,0:T(8,128)(2,1)} %param.8), channel_id=1, replica_groups=mesh['pages'=16,'tok'=2] {'pages'}, dimensions={0}, use_global_device_ids=true | all-gather | bytes 278528 | tf_op jit(solution)/shard_map/all_gather | solution.py:39
  32.1 0.0 copy-done
  32.1 1.2 %while.35 = (s32[]{:T(128)}, f32[1024,1]{0,1:T(1,128)S(1)}, bf16[1024,128]{1,0:T(8,128)(2,1)S(1)}, bf16[1,512,128]{2,1,0:T(8,128)(2,1)S(1)}, s32[]{:T(128)}, /*i...) while((s32[]{:T(128)}, f32[1024,1]{0,1:T(1,128)S(1)}, ...), condition=%wide.region_3.4_spmd.clone, body=%wide.region_0.3_spmd.clone.sunk | while | flops 68420104 | bytes 2376867 | solution.py:67
  32.1 0.3 fusion.38
  32.4 0.2 exponential_reduce_fusion.2
  32.7 0.3 fusion.38
  33.0 0.2 exponential_reduce_fusion.2
  33.2 4.4 %all-gather = f32[2048,1]{0,1:T(1,128)S(1)} all-gather(f32[1024,1]{0,1:T(1,128)S(1)} %get-tuple-element.249), channel_id=2, replica_groups=mesh['pages'=16,'tok'=2] {'tok'}, dimensions={0}, use_global_device_ids=true | all-gather | bytes 12288 | tf_op jit(solution)/shard_map/all_gather | solution.py:18
  37.6 0.1 squeeze.28
  37.7 0.1 squeeze.29
  37.8 0.0 copy-start.2
  37.8 0.1 add_reduce_fusion
  37.9 0.5 copy-done.2
  38.4 0.6 fusion.24
  39.1 0.1 broadcast_in_dim.84
  39.2 0.1 broadcast_in_dim.85
  39.3 2.4 %while.36 = (s32[]{:T(128)}, f32[1024,128]{1,0:T(8,128)S(1)}, f32[1,512,128]{2,1,0:T(8,128)S(1)}, bf16[1024,128]{1,0:T(8,128)(2,1)S(1)}, bf16[1,512,128]{2,1,0:T...) while((s32[]{:T(128)}, f32[1024,128]{1,0:T(8,128)S(1)}, ...), condition=%wide.region_6.7_spmd.clone, body=%wide.region_5.6_spmd.clone.sunk | while | flops 203097088 | bytes 2897109 | solution.py:103
  39.4 0.4 fusion.45
  39.8 0.4 fusion.47
  40.2 0.3 fusion.46
  40.5 0.4 fusion.45
  41.0 0.4 fusion.47
  41.4 0.3 fusion.46
  41.7 0.0 copy-start.1
  41.7 0.8 copy-done.1
  42.5 0.0 reduce-scatter.2.cloned.1.call-update
  42.5 0.7 broadcast_multiply_fusion
  43.2 52.9 %reduce-scatter.2.cloned.1.call-done = f32[64,128]{1,0:T(8,128)} async-done(((f32[1024,128]{1,0:T(8,128)}), f32[64,128]{1,0:T(8,128)}) %reduce-scatter.2.cloned.1.call-update) | async-done | bytes 32784 | tf_op jit(solution)/shard_map/reduce_scatter | solution.py:105
  96.2 9.6 %psum.7 = f32[2,32,128]{2,1,0:T(8,128)} all-reduce(f32[2,32,128]{2,1,0:T(8,128)} %bitcast.50), channel_id=1, replica_groups=mesh['pages'=16,'tok'=2] {'tok'}, use_global_device_ids=true, to_apply=%region_8.9 | all-reduce | flops 8192 | bytes 65536 | tf_op jit(solution)/shard_map/psum | solution.py:106
  (15 shorter events, 0.3 us)
Async XLA Ops:
  7.2 89.0 %reduce-scatter.2.cloned.1.call-start = ((), (), s32[]{:S(2)}) async-start(), calls=%async_computation.1 | async-start | bytes 557056 | tf_op jit(solution)/shard_map/reduce_scatter | solution.py:105
  7.9 24.2 %copy-start = (bf16[1,512,128]{2,1,0:T(8,128)(2,1)S(1)}, bf16[1,512,128]{2,1,0:T(8,128)(2,1)}, u32[]{:S(2)}) copy-start(bf16[1,512,128]{2,1,0:T(8,128)(2,1)} %param.9) | copy-start | bytes 393220
  37.8 0.7 copy-start.2
  41.7 0.8 copy-start.1
Sparse Core Ops, SparseCore 0:
  42.6 53.4 reduce-scatter.1
where the time goes:
time: 113 us
  waiting for transfers between devices  52.9 us (47%)
  blocking collectives  38.1 us (34%)
  between operations  14.7 us (13%)
  matrix products  2.87 us (3%)
  other arithmetic  2.05 us (2%)
  local copies, waits for them, and re-layouts  1.7 us (2%)
    reduce_scatter x1, waiting for transfers between devices, on_device(): lax.psum_scatter(query_terms, 'pages', scatter_dimension=0, tiled=True)  52.9 us
    all_gather x1, blocking collectives, on_device(): gathered = lax.all_gather(queries, 'pages', axis=0, tiled=True)  24.2 us
    psum x1, blocking collectives, on_device(): owned = lax.psum(owned, 'tok')  9.55 us
    all_gather x1, blocking collectives, combined_all(): everything = lax.all_gather(value, axis)  4.36 us
  transfers between devices with their start and end apart: 1, of which 1 were waited for; matrix products, arithmetic and copies ran while one was open for 1% of the time, Pallas kernels for 0%

commit v1 on v0

v1 whole, which is shorter than its diff:
```python
import functools
import math

import jax
import jax.numpy as jnp
from jax import lax
from jax.experimental import pallas as pl
from jax.experimental.pallas import tpu as pltpu
from jax.sharding import PartitionSpec as P

MASKED = -1.0e30
LOGIT_SPAN = 8.0
CENTRE_SHIFT = 0.5
FILL_SHARE = 0.75
LANES = 128
ROW_BLOCK = 512
VMEM_BYTES = 24 * 2**20


def over_tokens(left, right):
    return lax.dot_general(left, right, (((0,), (0,)), ((), ())), preferred_element_type=jnp.float32)


def over_features(left, right):
    return lax.dot_general(left, right, (((1,), (1,)), ((), ())), preferred_element_type=jnp.float32)


def group_sums(values, width):
    lane = lax.broadcasted_iota(jnp.int32, values.shape, 1)
    step = 1
    while step < width:
        below = pltpu.roll(values, step, 1)
        above = pltpu.roll(values, LANES - step, 1)
        values = values + jnp.where((lane & step) != 0, below, above)
        step *= 2
    return values


def body(
    query_len, page_len, copies, limits_ref, rows_ref, mine_ref, other_ref, sign_ref,
    blocks_ref, own_ref, sent_ref, loss_ref, own_sum, other_sum,
):
    row_count, width = rows_ref.shape
    tokens = mine_ref.shape[0]
    scale = width ** (-0.5)
    rate = scale * math.log2(math.e)
    gain = LOGIT_SPAN / query_len
    centre = query_len * (CENTRE_SHIFT + math.log(FILL_SHARE * page_len))
    block_rows = math.gcd(row_count, ROW_BLOCK)
    block_count = row_count // block_rows
    pieces = block_rows // LANES
    mine = mine_ref[...]
    other = other_ref[...]

    def one_block(offset):
        query_rows = rows_ref[pl.ds(offset, block_rows), :]
        place = lax.broadcasted_iota(jnp.int32, (tokens, block_rows), 0)
        raw_own = jnp.where(place < limits_ref[0], over_features(mine, query_rows), MASKED)
        raw_other = jnp.where(place < limits_ref[1], over_features(other, query_rows), MASKED)
        highest = jnp.maximum(
            jnp.max(raw_own, axis=0, keepdims=True), jnp.max(raw_other, axis=0, keepdims=True)
        )
        exp_own = jnp.exp2((raw_own - highest) * rate)
        exp_other = jnp.exp2((raw_other - highest) * rate)
        total = jnp.sum(exp_own, axis=0, keepdims=True) + jnp.sum(exp_other, axis=0, keepdims=True)

        def stacked(v):
            return jnp.concatenate([v[:, LANES * k : LANES * (k + 1)] for k in range(pieces)], axis=0)

        sums = stacked(total)
        smooth = stacked(highest) * scale + jnp.log(sums)
        similarity = group_sums(smooth, query_len)
        sign = stacked(sign_ref[:, pl.ds(offset, block_rows)])
        against = -sign * (gain * (similarity - centre))
        small = jnp.exp(-jnp.abs(against))
        losses = jnp.maximum(against, 0.0) + jnp.log1p(small)
        sigmoid = jnp.where(against >= 0.0, 1.0, small) / (1.0 + small)
        factor = (-gain * sign) * sigmoid / sums
        factor = jnp.concatenate([factor[k : k + 1, :] for k in range(pieces)], axis=1)
        scaled_own = (exp_own * factor).astype(jnp.bfloat16)
        scaled_other = (exp_other * factor).astype(jnp.bfloat16)
        query_terms = over_tokens(mine, scaled_own) + over_tokens(other, scaled_other)
        query_terms = query_terms.T.astype(jnp.bfloat16)
        own_terms = jnp.dot(scaled_own, query_rows, preferred_element_type=jnp.float32)
        other_terms = jnp.dot(scaled_other, query_rows, preferred_element_type=jnp.float32)
        lane = lax.broadcasted_iota(jnp.int32, losses.shape, 1)
        loss = jnp.sum(jnp.where(lane % query_len == 0, losses, 0.0))
        return query_terms, own_terms, other_terms, loss

    dest_rows = blocks_ref.shape[2]
    dests = block_rows // dest_rows

    def put(index, query_terms):
        shaped = query_terms.reshape(dests, dest_rows, width)
        for k in range(copies):
            blocks_ref[pl.ds(index * dests, dests), k] = shaped

    if block_count == 1:
        query_terms, own_terms, other_terms, loss = one_block(0)
        put(0, query_terms)
    else:
        own_sum[...] = jnp.zeros_like(own_sum)
        other_sum[...] = jnp.zeros_like(other_sum)

        def step(index, loss_so_far):
            query_terms, own_terms, other_terms, loss = one_block(pl.multiple_of(index * block_rows, block_rows))
            put(index, query_terms)
            own_sum[...] += own_terms
            other_sum[...] += other_terms
            return loss_so_far + loss

        loss = lax.fori_loop(0, block_count, step, jnp.float32(0.0))
        own_terms = own_sum[...]
        other_terms = other_sum[...]
    own_ref[...] = own_terms * scale
    sent_ref[pl.ds(0, tokens), :] = (other_terms * scale).astype(jnp.bfloat16)
    loss_all = jnp.full(loss_ref.shape, loss, jnp.float32)
    loss_ref[...] = loss_all
    tail = sent_ref.shape[0] - tokens
    whole = jnp.full((tail, width), loss, jnp.float32)
    high = whole.astype(jnp.bfloat16)
    rest = whole - high.astype(jnp.float32)
    middle = rest.astype(jnp.bfloat16)
    low = (rest - middle.astype(jnp.float32)).astype(jnp.bfloat16)
    lane = lax.broadcasted_iota(jnp.int32, (tail, width), 1)
    parts = jnp.where(
        lane == 0,
        high.astype(jnp.float32),
        jnp.where(lane == 1, middle.astype(jnp.float32), low.astype(jnp.float32)),
    )
    sent_ref[pl.ds(tokens, tail), :] = parts.astype(jnp.bfloat16)


def on_device(queries, pages, pad_counts, labels):
    query_count, query_len, width = queries.shape
    _, tokens, _ = pages.shape
    owners = lax.axis_size("pages")
    shares = lax.axis_size("tok")
    if shares != 2 or query_count % shares:
        raise ValueError("unsupported split")
    share = lax.axis_index("tok")
    page_len = tokens * shares
    picked = query_count // shares
    dest_rows = picked * query_len
    swap = [(0, 1), (1, 0)]

    mine = pages[0]
    other = lax.ppermute(mine, "tok", swap)
    chosen = lax.dynamic_slice_in_dim(queries, share * picked, picked, 0).reshape(1, dest_rows, width)
    gathered = lax.all_to_all(
        jnp.broadcast_to(chosen, (owners, dest_rows, width)), "pages", 0, 0, tiled=True
    )
    rows = gathered.reshape(owners * dest_rows, width)
    usable = page_len - pad_counts[0]
    limits = jnp.stack([usable - share * tokens, usable - (1 - share) * tokens])
    label = lax.dynamic_slice_in_dim(labels.reshape(owners, query_count), share * picked, picked, 1)
    sign = jnp.repeat(2.0 * label.reshape(owners * picked).astype(jnp.float32) - 1.0, query_len)[None, :]

    row_count = owners * dest_rows
    tail = 16
    vmem = pl.BlockSpec(memory_space=pltpu.VMEM)
    blocks, own, sent, loss = pl.pallas_call(
        functools.partial(body, query_len, page_len, shares),
        out_shape=(
            jax.ShapeDtypeStruct((owners, shares, dest_rows, width), jnp.bfloat16),
            jax.ShapeDtypeStruct((tokens, width), jnp.float32),
            jax.ShapeDtypeStruct((tokens + tail, width), jnp.bfloat16),
            jax.ShapeDtypeStruct((8, LANES), jnp.float32),
        ),
        in_specs=[pl.BlockSpec(memory_space=pltpu.SMEM), vmem, vmem, vmem, vmem],
        out_specs=(vmem, vmem, vmem, vmem),
        scratch_shapes=[pltpu.VMEM((tokens, width), jnp.float32)] * 2,
        cost_estimate=pl.CostEstimate(
            flops=6 * row_count * page_len * width,
            transcendentals=row_count * page_len,
            bytes_accessed=4 * row_count * width + 10 * tokens * width,
        ),
        compiler_params=pltpu.CompilerParams(vmem_limit_bytes=VMEM_BYTES),
        name="page_step",
    )(limits, rows, mine, other, sign)

    partials = lax.all_to_all(
        blocks.reshape(owners * shares, dest_rows, width), ("pages", "tok"), 0, 0, tiled=True
    )
    received = lax.ppermute(sent, "tok", swap)
    page_grad = (own + received[:tokens].astype(jnp.float32))[None]
    extra = received[tokens, :3].astype(jnp.float32)
    page_loss = loss[0, :1] + (extra[0] + extra[1] + extra[2])
    summed = jnp.sum(
        partials.reshape(owners, shares, dest_rows, width).astype(jnp.float32), axis=0
    ) * (width ** (-0.5))
    query_grad = summed.reshape(query_count, query_len, width)
    return query_grad, page_grad, page_loss


def solution(mesh):
    return jax.shard_map(
        on_device,
        mesh=mesh,
        in_specs=(P("pages", None, None), P("pages", "tok", None), P("pages"), P(None, "pages")),
        out_specs=(P("pages", None, None), P("pages", "tok", None), P("pages")),
        check_vma=False,
    )
```

time: 113 us -> 38.2 us (0.34)
  waiting for transfers between devices: 52.9 us -> 10.6 us
  blocking collectives: 38.1 us -> 0 us
  starting transfers between devices: 0.04 us -> 13.3 us
  between operations: 14.7 us -> 5.13 us
  Pallas kernels: 0 us -> 3.02 us
  matrix products: 2.87 us -> 0 us
  local copies, waits for them, and re-layouts: 1.7 us -> 3.32 us
    reduce_scatter x1 -> x0, waiting for transfers between devices: 52.9 us -> none  [on_device(): lax.psum_scatter(query_terms, 'pages', scatter_dimension=0, tiled=True)]
    all_gather x2 -> x0, blocking collectives: 28.5 us -> none  [the longest x1 24.2 us: on_device(): gathered = lax.all_gather(queries, 'pages', axis=0, tiled=True)]
    all_to_all x0 -> x2, starting transfers between devices: none -> 10.2 us  [the longest x1 7.52 us: on_device(): lax.all_to_all(jnp.broadcast_to(chosen, (owners, dest_rows, width)), 'pag...]
    psum x1 -> x0, blocking collectives: 9.55 us -> none  [on_device(): owned = lax.psum(owned, 'tok')]
    all_to_all x0 -> x2, waiting for transfers between devices: none -> 8.37 us  [the longest x1 6.36 us: on_device(): lax.all_to_all(blocks.reshape(owners * shares, dest_rows, width), ('pages...]
    ppermute x0 -> x2, starting transfers between devices: none -> 3.1 us  [the longest x1 1.58 us: on_device(): other = lax.ppermute(mine, 'tok', swap)]
    pallas_call x0 -> x1, Pallas kernels: none -> 3.02 us  [on_device(): pl.pallas_call(functools.partial(body, query_len, page_len, shares), out_...]
    dot_general x8 -> x0, matrix products: 2.87 us -> none  [the longest x4 1.52 us: scores_for(): lax.dot_general(query_block, pages[page_no], (((1,), (1,)), ((), ())), pr...]
  transfers between devices with their start and end apart: 1 -> 4, of which waited for: 1 -> 4; matrix products, arithmetic and copies ran while one was open for 1% -> 9% of each run, Pallas kernels for 0% -> 0%
where the time goes in v1:
time: 38.2 us; the launch traced here: 37.7 us
  starting transfers between devices  13.3 us (35%)
  waiting for transfers between devices  10.6 us (28%)
  between operations  5.13 us (13%)
  local copies, waits for them, and re-layouts  3.32 us (9%)
  Pallas kernels  3.02 us (8%)
  other arithmetic  2.32 us (6%)
    all_to_all x1, starting transfers between devices, on_device(): lax.all_to_all(jnp.broadcast_to(chosen, (owners, dest_rows, width)), 'pag...  7.52 us
    all_to_all x1, waiting for transfers between devices, on_device(): lax.all_to_all(blocks.reshape(owners * shares, dest_rows, width), ('pages...  6.36 us
    pallas_call x1, Pallas kernels, on_device(): pl.pallas_call(functools.partial(body, query_len, page_len, shares), out_...  3.02 us
    all_to_all x1, starting transfers between devices, on_device(): lax.all_to_all(blocks.reshape(owners * shares, dest_rows, width), ('pages...  2.7 us
    all_to_all x1, waiting for transfers between devices, on_device(): lax.all_to_all(jnp.broadcast_to(chosen, (owners, dest_rows, width)), 'pag...  2.01 us
    ppermute x1, waiting for transfers between devices, on_device(): other = lax.ppermute(mine, 'tok', swap)  1.94 us
    ppermute x1, starting transfers between devices, on_device(): other = lax.ppermute(mine, 'tok', swap)  1.58 us
    ppermute x1, starting transfers between devices, on_device(): received = lax.ppermute(sent, 'tok', swap)  1.52 us
  transfers between devices with their start and end apart: 4, of which 4 were waited for; matrix products, arithmetic and copies ran while one was open for 9% of the time, Pallas kernels for 0%

profile of v1, /device:TPU:0, one launch (start us, length us, event | category | flops | bytes accessed | tf_op | source)
XLA Modules:
  0.0 37.7 jit_solution(4494045376462885563)
XLA Ops:
  0.6 0.0 copy-start
  0.6 0.7 %copy-done = bf16[2,32,128]{2,1,0:T(8,128)(2,1)S(1)} copy-done((bf16[2,32,128]{2,1,0:T(8,128)(2,1)S(1)}, bf16[2,32,128]{2,1,0:T(8,128)(2,1)}, u32[]{:S(2)}) %copy-start) | copy-done | bytes 16408
  1.4 0.7 %broadcast_in_dim.14 = bf16[16,32,128]{2,1,0:T(8,128)(2,1)} broadcast(bf16[32,128]{1,0:T(8,128)(2,1)S(1)} %dynamic-slice_bitcast_fusion), dimensions={1,2} | broadcast | bytes 139264 | tf_op jit(solution)/shard_map/broadcast_in_dim | solution.py:151
  2.0 0.0 copy-start.1
  2.0 7.5 %all-to-all-start = ((bf16[16,32,128]{2,1,0:T(8,128)(2,1)}), bf16[16,32,128]{2,1,0:T(8,128)(2,1)S(1)}, u32[]{:S(2)}, u32[]{:S(2)}) async-start(bf16[16,32,128]{2,1,0:T(8,128)(2,1)} %broadcast_in_dim.14), calls=%async_computation | async-start | bytes 262144 | tf_op jit(solution)/shard_map/all_to_all | solution.py:150
  9.6 0.0 copy-done.1
  9.6 0.0 copy-start.2
  9.6 1.6 %collective-permute-start = (bf16[512,128]{1,0:T(8,128)(2,1)S(1)}, bf16[512,128]{1,0:T(8,128)(2,1)S(1)}, u32[]{:S(2)}, u32[]{:S(2)}) collective-permute-start(bf16[512,128]{1,0:T(8,128)(2,1)S(1)} %bitcast.15), channel_id=1, source_target_pairs={{0,1},{1,0},{2,3},{3,2},{4,5},{5,4},{6,7},{7,6},{8,9},{9,8},{10,11... | collective-permute-start | bytes 393224 | tf_op jit(solution)/shard_map/ppermute | solution.py:148
  11.2 0.5 %broadcast.19 = s32[]{:T(128)} broadcast(s32[]{:T(128)} %constant.6.clone.1), dimensions={} | broadcast | bytes 8 | tf_op args[3]
  11.7 0.0 copy-done.2
  11.7 0.7 %reduce.5 = s32[32]{0:T(128)S(1)} reduce(s32[32,1]{0,1:T(1,128)S(1)} %copy-done.2, s32[]{:T(128)} %broadcast.19), dimensions={1}, to_apply=%param.7.reduce_sub_computation.3 | reduce | bytes 260 | tf_op args[3]
  12.3 0.1 reshape.38
  12.4 0.2 add_reduce_fusion
  12.6 0.1 broadcast_in_dim.15
  12.7 0.1 broadcast_in_dim_reshape.3.sign_ref
  13.4 0.1 pad_add_fusion.limits_ref
  13.5 1.9 %collective-permute-done.other_ref = bf16[512,128]{1,0:T(8,128)(2,1)S(1)} collective-permute-done((bf16[512,128]{1,0:T(8,128)(2,1)S(1)}, bf16[512,128]{1,0:T(8,128)(2,1)S(1)}, u32[]{:S(2)}, u32[]{:S(2)}) %collective-permute-start) | collective-permute-done | bytes 131104 | tf_op jit(solution)/shard_map/ppermute | solution.py:148
  15.5 2.0 %all-to-all-done = bf16[16,32,128]{2,1,0:T(8,128)(2,1)S(1)} async-done(((bf16[16,32,128]{2,1,0:T(8,128)(2,1)}), bf16[16,32,128]{2,1,0:T(8,128)(2,1)S(1)}, u32[]{:S(2)}, u32[]{:S(2)}) %all-to-all-start) | async-done | bytes 131104 | tf_op jit(solution)/shard_map/all_to_all | solution.py:150
  17.5 3.0 %page_step.1 = (bf16[16,2,32,128]{3,2,1,0:T(8,128)(2,1)}, f32[512,128]{1,0:T(8,128)S(1)}, bf16[528,128]{1,0:T(8,128)(2,1)S(1)}, f32[8,128]{1,0:T(8,128)S(1)}) custom-call(s32[2]{0:T(128)S(1)} %pad_add_fusion.limits_ref, bf16[512,128]{1,0:T(8,128)(2,1)S(1)} %bitcast.14, bf16[512,128]{1,0:T(8,128)(2,1)S(1)} %bitcast.16, ...), custom_call_target="tpu_custom_call" | custom-call | flops 402653184 | bytes 917504 | tf_op jit(solution)/shard_map/page_step/pallas_call | solution.py:162
  20.5 1.5 %collective-permute-start.1 = (bf16[528,128]{1,0:T(8,128)(2,1)S(1)}, bf16[528,128]{1,0:T(8,128)(2,1)S(1)}, u32[]{:S(2)}, u32[]{:S(2)}) collective-permute-start(bf16[528,128]{1,0:T(8,128)(2,1)S(1)} %get-tuple-element.9), channel_id=1, source_target_pairs={{0,1},{1,0},{2,3},{3,2},{4,5},{5,4},{6,7},{7,6},{8,9},{9,8},{10,11... | collective-permute-start | bytes 405512 | tf_op jit(solution)/shard_map/ppermute | solution.py:185
  22.0 0.5 %slice.22 = f32[1,1]{1,0:T(1,128)} slice(f32[8,128]{1,0:T(8,128)S(1)} %get-tuple-element.10), slice={[0:1], [0:1]} | slice | bytes 8 | tf_op jit(solution)/shard_map/slice | solution.py:188
  22.5 2.7 %all-to-all-start.1 = ((bf16[32,32,128]{2,1,0:T(8,128)(2,1)}), bf16[32,32,128]{2,1,0:T(8,128)(2,1)S(1)}, u32[]{:S(2)}, u32[]{:S(2)}) async-start(bf16[32,32,128]{2,1,0:T(8,128)(2,1)} %bitcast.6), calls=%async_computation.1 | async-start | bytes 524288 | tf_op jit(solution)/shard_map/all_to_all | solution.py:182
  25.2 0.3 collective-permute-done.1
  25.5 0.7 %fusion = (f32[1,1]{1,0:T(1,128)}, f32[1,1]{1,0:T(1,128)}, f32[1,1]{1,0:T(1,128)}) fusion(f32[1,3]{1,0:T(1,128)S(1)} %slice_convert_fusion), kind=kLoop, calls=%fused_computation.7 | loop fusion | bytes 24 | tf_op jit(solution)/shard_map/slice | solution.py:188
  28.8 0.7 %add_bitcast_fusion = f32[1,512,128]{2,1,0:T(8,128)} fusion(f32[512,128]{1,0:T(8,128)S(1)} %get-tuple-element.8, bf16[528,128]{1,0:T(8,128)(2,1)S(1)} %collective-permute-done.1), kind=kLoop, calls=%fused_computation.1 | loop fusion | flops 131072 | bytes 655360 | tf_op jit(solution)/shard_map/broadcast_in_dim | solution.py:186
  29.5 6.4 %all-to-all-done.1 = bf16[32,32,128]{2,1,0:T(8,128)(2,1)S(1)} async-done(((bf16[32,32,128]{2,1,0:T(8,128)(2,1)}), bf16[32,32,128]{2,1,0:T(8,128)(2,1)S(1)}, u32[]{:S(2)}, u32[]{:S(2)}) %all-to-all-start.1) | async-done | bytes 262176 | tf_op jit(solution)/shard_map/all_to_all | solution.py:182
  35.9 0.6 %broadcast_multiply_fusion = f32[2,32,128]{2,1,0:T(8,128)} fusion(f32[2,32,128]{2,1,0:T(8,128)S(1)} %convert_reduce_fusion), kind=kLoop, calls=%fused_computation.2 | loop fusion | flops 8192 | bytes 65536 | tf_op jit(solution)/shard_map/mul | solution.py:189
  (3 shorter events, 0.0 us)
Async XLA Ops:
  0.6 0.7 %copy-start = (bf16[2,32,128]{2,1,0:T(8,128)(2,1)S(1)}, bf16[2,32,128]{2,1,0:T(8,128)(2,1)}, u32[]{:S(2)}) copy-start(bf16[2,32,128]{2,1,0:T(8,128)(2,1)} %param.4) | copy-start | bytes 49156
  2.0 7.5 %copy-start.1 = (bf16[1,512,128]{2,1,0:T(8,128)(2,1)S(1)}, bf16[1,512,128]{2,1,0:T(8,128)(2,1)}, u32[]{:S(2)}) copy-start(bf16[1,512,128]{2,1,0:T(8,128)(2,1)} %param.5) | copy-start | bytes 393220
  2.0 15.4 %all-to-all-start = ((bf16[16,32,128]{2,1,0:T(8,128)(2,1)}), bf16[16,32,128]{2,1,0:T(8,128)(2,1)S(1)}, u32[]{:S(2)}, u32[]{:S(2)}) async-start(bf16[16,32,128]{2,1,0:T(8,128)(2,1)} %broadcast_in_dim.14), calls=%async_computation | async-start | bytes 262144 | tf_op jit(solution)/shard_map/all_to_all | solution.py:150
  9.6 2.1 %copy-start.2 = (s32[32,1]{0,1:T(1,128)S(1)}, s32[32,1]{0,1:T(1,128)}, u32[]{:S(2)}) copy-start(s32[32,1]{0,1:T(1,128)} %param.7) | copy-start | bytes 388
  9.6 5.9 %collective-permute-start = (bf16[512,128]{1,0:T(8,128)(2,1)S(1)}, bf16[512,128]{1,0:T(8,128)(2,1)S(1)}, u32[]{:S(2)}, u32[]{:S(2)}) collective-permute-start(bf16[512,128]{1,0:T(8,128)(2,1)S(1)} %bitcast.15), channel_id=1, source_target_pairs={{0,1},{1,0},{2,3},{3,2},{4,5},{5,4},{6,7},{7,6},{8,9},{9,8},{10,11... | collective-permute-start | bytes 393224 | tf_op jit(solution)/shard_map/ppermute | solution.py:148
  20.5 5.0 %collective-permute-start.1 = (bf16[528,128]{1,0:T(8,128)(2,1)S(1)}, bf16[528,128]{1,0:T(8,128)(2,1)S(1)}, u32[]{:S(2)}, u32[]{:S(2)}) collective-permute-start(bf16[528,128]{1,0:T(8,128)(2,1)S(1)} %get-tuple-element.9), channel_id=1, source_target_pairs={{0,1},{1,0},{2,3},{3,2},{4,5},{5,4},{6,7},{7,6},{8,9},{9,8},{10,11... | collective-permute-start | bytes 405512 | tf_op jit(solution)/shard_map/ppermute | solution.py:185
  22.5 13.4 %all-to-all-start.1 = ((bf16[32,32,128]{2,1,0:T(8,128)(2,1)}), bf16[32,32,128]{2,1,0:T(8,128)(2,1)S(1)}, u32[]{:S(2)}, u32[]{:S(2)}) async-start(bf16[32,32,128]{2,1,0:T(8,128)(2,1)} %bitcast.6), calls=%async_computation.1 | async-start | bytes 524288 | tf_op jit(solution)/shard_map/all_to_all | solution.py:182

commit v2 on v1

v2 whole, which is shorter than its diff:
```python
import functools
import math

import jax
import jax.numpy as jnp
from jax import lax
from jax.experimental import pallas as pl
from jax.experimental.pallas import tpu as pltpu
from jax.sharding import PartitionSpec as P


MASKED = -1.0e30
LOGIT_SPAN = 8.0
CENTRE_SHIFT = 0.5
FILL_SHARE = 0.75
LANES = 128
ROW_BLOCK = 256
TAIL = 16
VMEM_BYTES = 24 * 2**20


def over_tokens(left, right):
    return lax.dot_general(left, right, (((0,), (0,)), ((), ())), preferred_element_type=jnp.float32)


def over_features(left, right):
    return lax.dot_general(left, right, (((1,), (1,)), ((), ())), preferred_element_type=jnp.float32)


def group_sums(values, width):
    lane = lax.broadcasted_iota(jnp.int32, values.shape, 1)
    step = 1
    while step < width:
        below = pltpu.roll(values, step, 1)
        above = pltpu.roll(values, LANES - step, 1)
        values = values + jnp.where((lane & step) != 0, below, above)
        step *= 2
    return values


def loss_parts(loss):
    whole = jnp.full((TAIL, LANES), loss, jnp.float32)
    high = whole.astype(jnp.bfloat16).astype(jnp.float32)
    middle = (whole - high).astype(jnp.bfloat16).astype(jnp.float32)
    low = whole - high - middle
    lane = lax.broadcasted_iota(jnp.int32, (TAIL, LANES), 1)
    parts = jnp.where(lane == 0, high, jnp.where(lane == 1, middle, jnp.where(lane == 2, low, 0.0)))
    return parts.astype(jnp.bfloat16)


def loss_of(parts):
    return jnp.sum(parts.astype(jnp.float32)[:1])


def step_body(
    query_len, page_len, copies, limits_ref, rows_ref, near_ref, far_ref, near2_ref, far2_ref, sign_ref,
    blocks_ref, near_out, far_out, sent_ref, loss_ref, *sums,
):
    row_count, width = rows_ref.shape
    tokens = near_ref.shape[0]
    scale = width ** (-0.5)
    rate = scale * math.log2(math.e)
    gain = LOGIT_SPAN / query_len
    centre = query_len * (CENTRE_SHIFT + math.log(FILL_SHARE * page_len))
    block_rows = math.gcd(row_count, ROW_BLOCK)
    block_count = row_count // block_rows
    pieces = block_rows // LANES

    def one_page(page, query_rows, near, far, offset):
        place = lax.broadcasted_iota(jnp.int32, (tokens, block_rows), 0)
        raw_near = jnp.where(place < limits_ref[2 * page], over_features(near, query_rows), MASKED)
        raw_far = jnp.where(place < limits_ref[2 * page + 1], over_features(far, query_rows), MASKED)
        highest = jnp.maximum(
            jnp.max(raw_near, axis=0, keepdims=True), jnp.max(raw_far, axis=0, keepdims=True)
        )
        exp_near = jnp.exp2((raw_near - highest) * rate)
        exp_far = jnp.exp2((raw_far - highest) * rate)
        total = jnp.sum(exp_near, axis=0, keepdims=True) + jnp.sum(exp_far, axis=0, keepdims=True)

        def stacked(v):
            return jnp.concatenate([v[:, LANES * k : LANES * (k + 1)] for k in range(pieces)], axis=0)

        sums = stacked(total)
        smooth = stacked(highest) * scale + jnp.log(sums)
        similarity = group_sums(smooth, query_len)
        sign = stacked(sign_ref[page : page + 1, pl.ds(offset, block_rows)])
        against = -sign * (gain * (similarity - centre))
        small = jnp.exp(-jnp.abs(against))
        losses = jnp.maximum(against, 0.0) + jnp.log1p(small)
        sigmoid = jnp.where(against >= 0.0, 1.0, small) / (1.0 + small)
        factor = (-gain * sign) * sigmoid / sums
        factor = jnp.concatenate([factor[k : k + 1, :] for k in range(pieces)], axis=1)
        scaled_near = (exp_near * factor).astype(jnp.bfloat16)
        scaled_far = (exp_far * factor).astype(jnp.bfloat16)
        query_terms = over_tokens(near, scaled_near) + over_tokens(far, scaled_far)
        near_terms = jnp.dot(scaled_near, query_rows, preferred_element_type=jnp.float32)
        far_terms = jnp.dot(scaled_far, query_rows, preferred_element_type=jnp.float32)
        lane = lax.broadcasted_iota(jnp.int32, losses.shape, 1)
        loss = jnp.sum(jnp.where(lane % query_len == 0, losses, 0.0))
        return query_terms, near_terms, far_terms, loss

    def one_block(offset):
        query_rows = rows_ref[pl.ds(offset, block_rows), :]
        terms, *first = one_page(0, query_rows, near_ref[...], far_ref[...], offset)
        terms2, *second = one_page(1, query_rows, near2_ref[...], far2_ref[...], offset)
        return (terms + terms2).T.astype(jnp.bfloat16), first, second

    dest_rows = blocks_ref.shape[2]
    dests = block_rows // dest_rows

    def put(index, query_terms):
        shaped = query_terms.reshape(dests, dest_rows, width)
        for k in range(copies):
            blocks_ref[pl.ds(index * dests, dests), k] = shaped

    if block_count == 1:
        query_terms, (near_sum, far_sum, loss), (near2_sum, far2_sum, loss2) = one_block(0)
        put(0, query_terms)
    else:
        for ref in sums:
            ref[...] = jnp.zeros_like(ref)

        def step(index, so_far):
            query_terms, first, second = one_block(pl.multiple_of(index * block_rows, block_rows))
            put(index, query_terms)
            for ref, value in zip(sums, (first[0], first[1], second[0], second[1])):
                ref[...] += value
            return so_far[0] + first[2], so_far[1] + second[2]

        loss, loss2 = lax.fori_loop(0, block_count, step, (jnp.float32(0.0), jnp.float32(0.0)))
        near_sum, far_sum, near2_sum, far2_sum = (ref[...] for ref in sums)
    near_out[...] = near_sum * scale
    far_out[...] = far_sum * scale
    sent_ref[pl.ds(0, tokens), :] = (near2_sum * scale).astype(jnp.bfloat16)
    sent_ref[pl.ds(tokens, tokens), :] = (far2_sum * scale).astype(jnp.bfloat16)
    sent_ref[pl.ds(2 * tokens, TAIL), :] = loss_parts(loss2)
    loss_ref[...] = jnp.full(loss_ref.shape, loss, jnp.float32)


def merge_body(far_ref, loss_ref, got_ref, sent_ref):
    tokens = far_ref.shape[0]
    total = far_ref[...] + got_ref[pl.ds(tokens, tokens), :].astype(jnp.float32)
    sent_ref[pl.ds(0, tokens), :] = total.astype(jnp.bfloat16)
    loss = jnp.max(loss_ref[...]) + loss_of(got_ref[pl.ds(2 * tokens, TAIL), :])
    sent_ref[pl.ds(tokens, TAIL), :] = loss_parts(loss)


def last_body(near_ref, loss_ref, got_ref, got2_ref, grad_ref, total_ref):
    tokens = near_ref.shape[0]
    grad_ref[0] = (
        near_ref[...]
        + got_ref[pl.ds(0, tokens), :].astype(jnp.float32)
        + got2_ref[pl.ds(0, tokens), :].astype(jnp.float32)
    )
    total_ref[0] = (
        jnp.max(loss_ref[...])
        + loss_of(got_ref[pl.ds(2 * tokens, TAIL), :])
        + loss_of(got2_ref[pl.ds(tokens, TAIL), :])
    )


def device_step(queries, pages, pad_counts, labels):
    query_count, query_len, width = queries.shape
    _, tokens, _ = pages.shape
    owners = lax.axis_size("pages")
    shares = lax.axis_size("tok")
    if shares != 2 or query_count % shares or owners % 2:
        raise ValueError("unsupported split")
    share = lax.axis_index("tok")
    side = lax.axis_index("pages") % 2
    page_len = tokens * shares
    picked = query_count // shares
    dest_rows = picked * query_len
    chips = owners // 2
    swap = [(0, 1), (1, 0)]
    partner = [(i, i ^ 1) for i in range(owners)]
    same_side = [[2 * j + c for j in range(chips)] for c in range(2)]
    same_side_all = [
        [(2 * j + c) * shares + k for j in range(chips) for k in range(shares)] for c in range(2)
    ]
    vmem = pl.BlockSpec(memory_space=pltpu.VMEM)
    smem = pl.BlockSpec(memory_space=pltpu.SMEM)
    params = pltpu.CompilerParams(vmem_limit_bytes=VMEM_BYTES)

    chosen = lax.dynamic_slice_in_dim(queries, share * picked, picked, 0).reshape(1, dest_rows, width)
    rows = lax.all_to_all(
        jnp.broadcast_to(chosen, (chips, dest_rows, width)),
        "pages", 0, 0, tiled=True, axis_index_groups=same_side,
    ).reshape(chips * dest_rows, width)

    near = pages[0]
    far = lax.ppermute(near, "tok", swap)
    near2 = lax.ppermute(near, "pages", partner)
    far2 = lax.ppermute(far, "pages", partner)
    facts = jnp.concatenate([labels[:, 0], pad_counts])
    facts2 = lax.ppermute(facts, "pages", partner)
    both = jnp.stack([facts, facts2])
    usable = page_len - both[:, -1:]
    limits = jnp.concatenate([usable - share * tokens, usable - (1 - share) * tokens], axis=1).reshape(4)
    label = both[:, :-1].reshape(2, chips, 2, shares, picked)
    label = lax.dynamic_slice(label, (0, 0, side, share, 0), (2, chips, 1, 1, picked))
    sign = jnp.repeat(2.0 * label.reshape(2, chips * picked).astype(jnp.float32) - 1.0, query_len, axis=1)

    row_count = chips * dest_rows
    block_rows = math.gcd(row_count, ROW_BLOCK)
    scratch = [] if row_count == block_rows else [pltpu.VMEM((tokens, width), jnp.float32)] * 4
    blocks, near_sum, far_sum, sent, loss = pl.pallas_call(
        functools.partial(step_body, query_len, page_len, shares),
        out_shape=(
            jax.ShapeDtypeStruct((chips, shares, dest_rows, width), jnp.bfloat16),
            jax.ShapeDtypeStruct((tokens, width), jnp.float32),
            jax.ShapeDtypeStruct((tokens, width), jnp.float32),
            jax.ShapeDtypeStruct((2 * tokens + TAIL, width), jnp.bfloat16),
            jax.ShapeDtypeStruct((8, LANES), jnp.float32),
        ),
        in_specs=[smem, vmem, vmem, vmem, vmem, vmem, vmem],
        out_specs=(vmem,) * 5,
        scratch_shapes=scratch,
        cost_estimate=pl.CostEstimate(
            flops=12 * row_count * page_len * width,
            transcendentals=2 * row_count * page_len,
            bytes_accessed=6 * row_count * width + 20 * tokens * width,
        ),
        compiler_params=params,
        name="page_step",
    )(limits, rows, near, far, near2, far2, sign)

    got = lax.ppermute(sent, "pages", partner)
    partials = lax.all_to_all(
        blocks.reshape(chips * shares, dest_rows, width),
        ("pages", "tok"), 0, 0, tiled=True, axis_index_groups=same_side_all,
    )
    merged = pl.pallas_call(
        merge_body,
        out_shape=jax.ShapeDtypeStruct((tokens + TAIL, width), jnp.bfloat16),
        in_specs=[vmem, vmem, vmem],
        out_specs=vmem,
        cost_estimate=pl.CostEstimate(flops=tokens * width, transcendentals=0, bytes_accessed=8 * tokens * width),
        compiler_params=params,
        name="merge",
    )(far_sum, loss, got)
    got2 = lax.ppermute(merged, "tok", swap)
    page_grad, page_loss = pl.pallas_call(
        last_body,
        out_shape=(
            jax.ShapeDtypeStruct((1, tokens, width), jnp.float32),
            jax.ShapeDtypeStruct((1,), jnp.float32),
        ),
        in_specs=[vmem, vmem, vmem, vmem],
        out_specs=(vmem, smem),
        cost_estimate=pl.CostEstimate(flops=2 * tokens * width, transcendentals=0, bytes_accessed=12 * tokens * width),
        compiler_params=params,
        name="page_out",
    )(near_sum, loss, got, got2)
    summed = jnp.sum(
        partials.reshape(chips, shares, dest_rows, width).astype(jnp.float32), axis=0
    ) * (width ** (-0.5))
    query_grad = summed.reshape(query_count, query_len, width)
    return query_grad, page_grad, page_loss


def solution(mesh):
    return jax.shard_map(
        device_step,
        mesh=mesh,
        in_specs=(P("pages", None, None), P("pages", "tok", None), P("pages"), P(None, "pages")),
        out_specs=(P("pages", None, None), P("pages", "tok", None), P("pages")),
        check_vma=False,
    )
```

time: 38.2 us -> 40.1 us (1.050)
  waiting for transfers between devices: 10.6 us -> 16.9 us
  between operations: 5.13 us -> 1.36 us
  local copies, waits for them, and re-layouts: 3.32 us -> 1.64 us
  Pallas kernels: 3.02 us -> 4.55 us
  other arithmetic: 2.32 us -> 1.17 us
  starting transfers between devices: 13.3 us -> 14.1 us
    all_to_all x2, waiting for transfers between devices: 8.37 us -> 13.6 us  [the longest x1 7.69 us: device_step(): lax.all_to_all(blocks.reshape(chips * shares, dest_rows, width), ('pages'...]
    ppermute x2 -> x6, starting transfers between devices: 3.1 us -> 4.66 us  [the longest x1 2.58 us: device_step(): far = lax.ppermute(near, 'tok', swap)]
    pallas_call x1 -> x3, Pallas kernels: 3.02 us -> 4.55 us  [the longest x1 3.61 us: device_step(): pl.pallas_call(functools.partial(step_body, query_len, page_len, shares),...]
    slice x2 -> x0, local copies, waits for them, and re-layouts: 1.18 us -> none  [on_device(): page_loss = loss[0, :1] + (extra[0] + extra[1] + extra[2])]
    ppermute x2 -> x6, waiting for transfers between devices: 2.21 us -> 3.31 us  [the longest x1 3.3 us: device_step(): got2 = lax.ppermute(merged, 'tok', swap)]
    all_to_all x2, starting transfers between devices: 10.2 us -> 9.45 us  [the longest x1 5.94 us: device_step(): lax.all_to_all(jnp.broadcast_to(chosen, (chips, dest_rows, width)), 'page...]
    broadcast_in_dim x1 -> x0, other arithmetic: 0.73 us -> none  [on_device(): page_grad = (own + received[:tokens].astype(jnp.float32))[None]]
    unnamed x1 -> x0, other arithmetic: 0.66 us -> none
  transfers between devices with their start and end apart: 4 -> 8, of which waited for: 4 -> 3; matrix products, arithmetic and copies ran while one was open for 9% -> 5% of each run, Pallas kernels for 0% -> 0%
where the time goes in v2:
time: 40.1 us; the launch traced here: 39.8 us
  waiting for transfers between devices  16.9 us (42%)
  starting transfers between devices  14.1 us (35%)
  Pallas kernels  4.55 us (11%)
  local copies, waits for them, and re-layouts  1.64 us (4%)
  between operations  1.36 us (3%)
  other arithmetic  1.17 us (3%)
    all_to_all x1, waiting for transfers between devices, device_step(): lax.all_to_all(blocks.reshape(chips * shares, dest_rows, width), ('pages'...  7.69 us
    all_to_all x1, waiting for transfers between devices, device_step(): lax.all_to_all(jnp.broadcast_to(chosen, (chips, dest_rows, width)), 'page...  5.95 us
    all_to_all x1, starting transfers between devices, device_step(): lax.all_to_all(jnp.broadcast_to(chosen, (chips, dest_rows, width)), 'page...  5.94 us
    pallas_call x1, Pallas kernels, device_step(): pl.pallas_call(functools.partial(step_body, query_len, page_len, shares),...  3.61 us
    all_to_all x1, starting transfers between devices, device_step(): lax.all_to_all(blocks.reshape(chips * shares, dest_rows, width), ('pages'...  3.51 us
    ppermute x1, waiting for transfers between devices, device_step(): got2 = lax.ppermute(merged, 'tok', swap)  3.3 us
    ppermute x1, starting transfers between devices, device_step(): far = lax.ppermute(near, 'tok', swap)  2.58 us
    ppermute x1, starting transfers between devices, device_step(): got2 = lax.ppermute(merged, 'tok', swap)  1.16 us
  transfers between devices with their start and end apart: 8, of which 3 were waited for; matrix products, arithmetic and copies ran while one was open for 5% of the time, Pallas kernels for 0%

profile of v2, /device:TPU:0, one launch (start us, length us, event | category | flops | bytes accessed | tf_op | source)
XLA Modules:
  0.0 39.8 jit_solution(5885638606113963885)
XLA Ops:
  0.6 0.0 copy-start
  0.6 0.6 %collective-permute-start.2 = (bf16[512,128]{1,0:T(8,128)(2,1)}, bf16[512,128]{1,0:T(8,128)(2,1)S(1)}, u32[]{:S(2)}, u32[]{:S(2)}) collective-permute-start(bf16[512,128]{1,0:T(8,128)(2,1)} %bitcast.13), channel_id=1, source_target_pairs={{0,2},{2,0},{4,6},{6,4},{8,10},{10,8},{12,14},{14,12},{16,18},{18,... | collective-permute-start | bytes 393224 | tf_op jit(solution)/shard_map/ppermute | solution.py:193
  1.2 2.6 %collective-permute-start.1 = (bf16[512,128]{1,0:T(8,128)(2,1)}, bf16[512,128]{1,0:T(8,128)(2,1)S(1)}, u32[]{:S(2)}, u32[]{:S(2)}) collective-permute-start(bf16[512,128]{1,0:T(8,128)(2,1)} %bitcast.14), channel_id=1, source_target_pairs={{0,1},{1,0},{2,3},{3,2},{4,5},{5,4},{6,7},{7,6},{8,9},{9,8},{10,11... | collective-permute-start | bytes 393224 | tf_op jit(solution)/shard_map/ppermute | solution.py:192
  4.4 0.0 copy-start.2
  4.4 0.6 %copy-done.2 = s32[32,1]{0,1:T(1,128)S(1)} copy-done((s32[32,1]{0,1:T(1,128)S(1)}, s32[32,1]{0,1:T(1,128)}, u32[]{:S(2)}) %copy-start.2) | copy-done | bytes 152
  5.1 0.1 pad_add_fusion.2
  5.2 0.1 collective-permute-start
  5.3 0.0 copy-done
  5.3 0.6 %broadcast_in_dim.11 = bf16[8,32,128]{2,1,0:T(8,128)(2,1)} broadcast(bf16[32,128]{1,0:T(8,128)(2,1)S(1)} %dynamic-slice_bitcast_fusion), dimensions={1,2} | broadcast | bytes 73728 | tf_op jit(solution)/shard_map/broadcast_in_dim | solution.py:187
  6.0 0.0 copy-start.1
  6.0 5.9 %all-to-all-start = ((bf16[8,32,128]{2,1,0:T(8,128)(2,1)}), bf16[8,32,128]{2,1,0:T(8,128)(2,1)S(1)}, u32[]{:S(2)}, u32[]{:S(2)}) async-start(bf16[8,32,128]{2,1,0:T(8,128)(2,1)} %broadcast_in_dim.11), calls=%async_computation | async-start | bytes 131072 | tf_op jit(solution)/shard_map/all_to_all | solution.py:186
  11.9 0.1 fusion.2
  12.0 0.0 collective-permute-done
  12.0 0.0 collective-permute-done.1.far_ref
  12.0 0.1 collective-permute-start.3
  12.2 0.1 fusion.1
  12.2 0.1 pad_add_fusion.1
  12.3 0.1 reshape.30.limits_ref
  12.4 0.1 reshape.32
  12.5 0.2 add_reduce_fusion
  12.7 0.1 broadcast_in_dim.12
  12.8 0.1 reshape.33.sign_ref
  12.9 5.9 %all-to-all-done = bf16[8,32,128]{2,1,0:T(8,128)(2,1)S(1)} async-done(((bf16[8,32,128]{2,1,0:T(8,128)(2,1)}), bf16[8,32,128]{2,1,0:T(8,128)(2,1)S(1)}, u32[]{:S(2)}, u32[]{:S(2)}) %all-to-all-start) | async-done | bytes 65568 | tf_op jit(solution)/shard_map/all_to_all | solution.py:186
  18.8 0.0 collective-permute-done.2.near2_ref
  18.8 0.0 collective-permute-done.3.far2_ref
  18.8 0.0 copy-done.1
  18.8 3.6 %page_step.1 = (bf16[8,2,32,128]{3,2,1,0:T(8,128)(2,1)}, f32[512,128]{1,0:T(8,128)S(1)}, f32[512,128]{1,0:T(8,128)S(1)}, bf16[1040,128]{1,0:T(8,128)(2,1)S(1)}, f32[8,128]{1,0:T(8,128)S(1)}) custom-call(s32[4]{0:T(128)S(1)} %reshape.30.limits_ref, bf16[256,128]{1,0:T(8,128)(2,1)S(1)} %bitcast.12, bf16[512,128]{1,0:T(8,128)(2,1)S(1)} %bitcast.15, ...), custom_call_target="tpu_custom_call" | custom-call | flops 402653184 | bytes 1507328 | tf_op jit(solution)/shard_map/page_step/pallas_call | solution.py:207
  22.4 3.5 %all-to-all-start.1 = ((bf16[16,32,128]{2,1,0:T(8,128)(2,1)}), bf16[16,32,128]{2,1,0:T(8,128)(2,1)S(1)}, u32[]{:S(2)}, u32[]{:S(2)}) async-start(bf16[16,32,128]{2,1,0:T(8,128)(2,1)} %bitcast.6), calls=%async_computation.1 | async-start | bytes 262144 | tf_op jit(solution)/shard_map/all_to_all | solution.py:229
  26.0 0.1 collective-permute-start.4
  26.0 7.7 %all-to-all-done.1 = bf16[16,32,128]{2,1,0:T(8,128)(2,1)S(1)} async-done(((bf16[16,32,128]{2,1,0:T(8,128)(2,1)}), bf16[16,32,128]{2,1,0:T(8,128)(2,1)S(1)}, u32[]{:S(2)}, u32[]{:S(2)}) %all-to-all-start.1) | async-done | bytes 131104 | tf_op jit(solution)/shard_map/all_to_all | solution.py:229
  33.7 0.0 collective-permute-done.4.got_ref
  33.8 0.1 merge.1
  33.9 1.2 %collective-permute-start.5 = (bf16[528,128]{1,0:T(8,128)(2,1)S(1)}, bf16[528,128]{1,0:T(8,128)(2,1)S(1)}, u32[]{:S(2)}, u32[]{:S(2)}) collective-permute-start(bf16[528,128]{1,0:T(8,128)(2,1)S(1)} %merge.1), channel_id=1, source_target_pairs={{0,1},{1,0},{2,3},{3,2},{4,5},{5,4},{6,7},{7,6},{8,9},{9,8},{10,11... | collective-permute-start | bytes 405512 | tf_op jit(solution)/shard_map/ppermute | solution.py:242
  35.0 0.6 %broadcast_multiply_fusion = f32[2,32,128]{2,1,0:T(8,128)} fusion(f32[2,32,128]{2,1,0:T(8,128)S(1)} %convert_reduce_fusion), kind=kLoop, calls=%fused_computation.1 | loop fusion | flops 8192 | bytes 65536 | tf_op jit(solution)/shard_map/mul | solution.py:255
  35.7 3.3 %collective-permute-done.5.got2_ref = bf16[528,128]{1,0:T(8,128)(2,1)S(1)} collective-permute-done((bf16[528,128]{1,0:T(8,128)(2,1)S(1)}, bf16[528,128]{1,0:T(8,128)(2,1)S(1)}, u32[]{:S(2)}, u32[]{:S(2)}) %collective-permute-start.5) | collective-permute-done | bytes 135200 | tf_op jit(solution)/shard_map/ppermute | solution.py:242
  39.0 0.8 %page_out.1 = (f32[1,512,128]{2,1,0:T(8,128)}, f32[1]{0:T(128)}) custom-call(f32[512,128]{1,0:T(8,128)S(1)} %get-tuple-element.11.near_ref, f32[8,128]{1,0:T(8,128)S(1)} %get-tuple-element.12.loss_ref, bf16[1040,128]{1,0:T(8,128)(2,1)S(1)} %collective-permute-done.4.got_ref, bf16[528,128]{1,0:T(8,128)(2,1)S(1)} %collective-permute-done.5.got2_ref), custom_call_target="tpu_custom_call" | custom-call | flops 131072 | bytes 786432 | tf_op jit(solution)/shard_map/page_out/pallas_call | solution.py:243
  (3 shorter events, 0.0 us)
Async XLA Ops:
  0.6 4.7 %copy-start = (bf16[2,32,128]{2,1,0:T(8,128)(2,1)S(1)}, bf16[2,32,128]{2,1,0:T(8,128)(2,1)}, u32[]{:S(2)}) copy-start(bf16[2,32,128]{2,1,0:T(8,128)(2,1)} %param.4) | copy-start | bytes 49156
  0.6 18.2 %collective-permute-start.2 = (bf16[512,128]{1,0:T(8,128)(2,1)}, bf16[512,128]{1,0:T(8,128)(2,1)S(1)}, u32[]{:S(2)}, u32[]{:S(2)}) collective-permute-start(bf16[512,128]{1,0:T(8,128)(2,1)} %bitcast.13), channel_id=1, source_target_pairs={{0,2},{2,0},{4,6},{6,4},{8,10},{10,8},{12,14},{14,12},{16,18},{18,... | collective-permute-start | bytes 393224 | tf_op jit(solution)/shard_map/ppermute | solution.py:193
  1.2 10.8 %collective-permute-start.1 = (bf16[512,128]{1,0:T(8,128)(2,1)}, bf16[512,128]{1,0:T(8,128)(2,1)S(1)}, u32[]{:S(2)}, u32[]{:S(2)}) collective-permute-start(bf16[512,128]{1,0:T(8,128)(2,1)} %bitcast.14), channel_id=1, source_target_pairs={{0,1},{1,0},{2,3},{3,2},{4,5},{5,4},{6,7},{7,6},{8,9},{9,8},{10,11... | collective-permute-start | bytes 393224 | tf_op jit(solution)/shard_map/ppermute | solution.py:192
  4.4 0.7 %copy-start.2 = (s32[32,1]{0,1:T(1,128)S(1)}, s32[32,1]{0,1:T(1,128)}, u32[]{:S(2)}) copy-start(s32[32,1]{0,1:T(1,128)} %param.7) | copy-start | bytes 388
  5.2 6.8 %collective-permute-start = (s32[33]{0:T(128)S(1)}, s32[33]{0:T(128)S(1)}, u32[]{:S(2)}, u32[]{:S(2)}) collective-permute-start(s32[33]{0:T(128)S(1)} %pad_add_fusion.2), channel_id=1, source_target_pairs={{0,2},{2,0},{4,6},{6,4},{8,10},{10,8},{12,14},{14,12},{16,18},{18,... | collective-permute-start | bytes 404 | tf_op jit(solution)/shard_map/ppermute | solution.py:196
  6.0 12.9 %copy-start.1 = (bf16[1,512,128]{2,1,0:T(8,128)(2,1)S(1)}, bf16[1,512,128]{2,1,0:T(8,128)(2,1)}, u32[]{:S(2)}) copy-start(bf16[1,512,128]{2,1,0:T(8,128)(2,1)} %param.5) | copy-start | bytes 393220
  6.0 12.8 %all-to-all-start = ((bf16[8,32,128]{2,1,0:T(8,128)(2,1)}), bf16[8,32,128]{2,1,0:T(8,128)(2,1)S(1)}, u32[]{:S(2)}, u32[]{:S(2)}) async-start(bf16[8,32,128]{2,1,0:T(8,128)(2,1)} %broadcast_in_dim.11), calls=%async_computation | async-start | bytes 131072 | tf_op jit(solution)/shard_map/all_to_all | solution.py:186
  12.0 6.8 %collective-permute-start.3 = (bf16[512,128]{1,0:T(8,128)(2,1)S(1)}, bf16[512,128]{1,0:T(8,128)(2,1)S(1)}, u32[]{:S(2)}, u32[]{:S(2)}) collective-permute-start(bf16[512,128]{1,0:T(8,128)(2,1)S(1)} %collective-permute-done.1.far_ref), channel_id=1, source_target_pairs={{0,2},{2,0},{4,6},{6,4},{8,10},{10,8},{12,14},{14,12},{16,18},{18,... | collective-permute-start | bytes 393224 | tf_op jit(solution)/shard_map/ppermute | solution.py:194
  22.4 11.3 %all-to-all-start.1 = ((bf16[16,32,128]{2,1,0:T(8,128)(2,1)}), bf16[16,32,128]{2,1,0:T(8,128)(2,1)S(1)}, u32[]{:S(2)}, u32[]{:S(2)}) async-start(bf16[16,32,128]{2,1,0:T(8,128)(2,1)} %bitcast.6), calls=%async_computation.1 | async-start | bytes 262144 | tf_op jit(solution)/shard_map/all_to_all | solution.py:229
  26.0 7.8 %collective-permute-start.4 = (bf16[1040,128]{1,0:T(8,128)(2,1)S(1)}, bf16[1040,128]{1,0:T(8,128)(2,1)S(1)}, u32[]{:S(2)}, u32[]{:S(2)}) collective-permute-start(bf16[1040,128]{1,0:T(8,128)(2,1)S(1)} %get-tuple-element.13), channel_id=1, source_target_pairs={{0,2},{2,0},{4,6},{6,4},{8,10},{10,8},{12,14},{14,12},{16,18},{18,... | collective-permute-start | bytes 798728 | tf_op jit(solution)/shard_map/ppermute | solution.py:228
  33.9 5.1 %collective-permute-start.5 = (bf16[528,128]{1,0:T(8,128)(2,1)S(1)}, bf16[528,128]{1,0:T(8,128)(2,1)S(1)}, u32[]{:S(2)}, u32[]{:S(2)}) collective-permute-start(bf16[528,128]{1,0:T(8,128)(2,1)S(1)} %merge.1), channel_id=1, source_target_pairs={{0,1},{1,0},{2,3},{3,2},{4,5},{5,4},{6,7},{7,6},{8,9},{9,8},{10,11... | collective-permute-start | bytes 405512 | tf_op jit(solution)/shard_map/ppermute | solution.py:242

commit v3 on v2

v3 whole, which is shorter than its diff:
```python
import functools
import math

import jax
import jax.numpy as jnp
from jax import lax
from jax.experimental import pallas as pl
from jax.experimental.pallas import tpu as pltpu
from jax.sharding import PartitionSpec as P


MASKED = -1.0e30
LOGIT_SPAN = 8.0
CENTRE_SHIFT = 0.5
FILL_SHARE = 0.75
LANES = 128
ROW_BLOCK = 256
TAIL = 16
VMEM_BYTES = 24 * 2**20


def over_tokens(left, right):
    return lax.dot_general(left, right, (((0,), (0,)), ((), ())), preferred_element_type=jnp.float32)


def over_features(left, right):
    return lax.dot_general(left, right, (((1,), (1,)), ((), ())), preferred_element_type=jnp.float32)


def group_sums(values, width):
    lane = lax.broadcasted_iota(jnp.int32, values.shape, 1)
    step = 1
    while step < width:
        below = pltpu.roll(values, step, 1)
        above = pltpu.roll(values, LANES - step, 1)
        values = values + jnp.where((lane & step) != 0, below, above)
        step *= 2
    return values


def loss_parts(loss):
    whole = jnp.full((TAIL, LANES), loss, jnp.float32)
    high = whole.astype(jnp.bfloat16).astype(jnp.float32)
    middle = (whole - high).astype(jnp.bfloat16).astype(jnp.float32)
    low = whole - high - middle
    lane = lax.broadcasted_iota(jnp.int32, (TAIL, LANES), 1)
    parts = jnp.where(lane == 0, high, jnp.where(lane == 1, middle, jnp.where(lane == 2, low, 0.0)))
    return parts.astype(jnp.bfloat16)


def loss_of(parts):
    return jnp.sum(parts.astype(jnp.float32)[:1])


def ask_body(queries_ref, out_ref, sems):
    copies = [
        pltpu.make_async_copy(queries_ref, out_ref.at[k], sems.at[k]) for k in range(out_ref.shape[0])
    ]
    for copy in copies:
        copy.start()
    for copy in copies:
        copy.wait()


class Page:
    def __init__(self, query_len, page_len, query_rows, near, far, limit_near, limit_far, sign):
        tokens, width = near.shape
        block_rows = query_rows.shape[0]
        pieces = block_rows // LANES
        scale = width ** (-0.5)
        rate = scale * math.log2(math.e)
        gain = LOGIT_SPAN / query_len
        centre = query_len * (CENTRE_SHIFT + math.log(FILL_SHARE * page_len))
        place = lax.broadcasted_iota(jnp.int32, (tokens, block_rows), 0)
        raw_near = jnp.where(place < limit_near, over_features(near, query_rows), MASKED)
        raw_far = jnp.where(place < limit_far, over_features(far, query_rows), MASKED)
        highest = jnp.maximum(
            jnp.max(raw_near, axis=0, keepdims=True), jnp.max(raw_far, axis=0, keepdims=True)
        )
        self.exp_near = jnp.exp2((raw_near - highest) * rate)
        self.exp_far = jnp.exp2((raw_far - highest) * rate)
        total = jnp.sum(self.exp_near, axis=0, keepdims=True) + jnp.sum(self.exp_far, axis=0, keepdims=True)

        def stacked(v):
            return jnp.concatenate([v[:, LANES * k : LANES * (k + 1)] for k in range(pieces)], axis=0)

        sums = stacked(total)
        smooth = stacked(highest) * scale + jnp.log(sums)
        similarity = group_sums(smooth, query_len)
        sign = stacked(sign)
        against = -sign * (gain * (similarity - centre))
        small = jnp.exp(-jnp.abs(against))
        losses = jnp.maximum(against, 0.0) + jnp.log1p(small)
        sigmoid = jnp.where(against >= 0.0, 1.0, small) / (1.0 + small)
        factor = (-gain * sign) * sigmoid / sums
        self.factor = jnp.concatenate([factor[k : k + 1, :] for k in range(pieces)], axis=1)
        lane = lax.broadcasted_iota(jnp.int32, losses.shape, 1)
        self.loss = jnp.sum(jnp.where(lane % query_len == 0, losses, 0.0))

    def near(self):
        return (self.exp_near * self.factor).astype(jnp.bfloat16)

    def far(self):
        return (self.exp_far * self.factor).astype(jnp.bfloat16)


def in_blocks(row_count, body):
    block_rows = math.gcd(row_count, ROW_BLOCK)
    count = row_count // block_rows
    if count == 1:
        body(0, block_rows, True)
        return

    @pl.loop(0, count)
    def _(index):
        body(index, block_rows, index == 0)


def add_to(ref, value, first):
    if first is True:
        ref[...] = value
    else:
        ref[...] = jnp.where(first, 0.0, ref[...]) + value


def step_body(
    query_len, page_len, limits_ref, rows_ref, near_ref, far_ref, near2_ref, far2_ref, sign_ref,
    blocks_ref, near_sum, near2_sum, loss_ref, held, sem,
):
    row_count, width = rows_ref.shape
    copies, dest_rows = held.shape[1:3]
    out = pltpu.make_async_copy(held, blocks_ref, sem)

    def body(index, block_rows, first):
        offset = pl.multiple_of(index * block_rows, block_rows)
        query_rows = rows_ref[pl.ds(offset, block_rows), :]
        near, far, near2, far2 = near_ref[...], far_ref[...], near2_ref[...], far2_ref[...]
        one, two = (
            Page(
                query_len, page_len, query_rows, a, b, limits_ref[2 * k], limits_ref[2 * k + 1],
                sign_ref[k : k + 1, pl.ds(offset, block_rows)],
            )
            for k, (a, b) in enumerate(((near, far), (near2, far2)))
        )
        scaled, scaled2 = one.near(), two.near()
        terms = (
            over_tokens(near, scaled) + over_tokens(far, one.far())
            + over_tokens(near2, scaled2) + over_tokens(far2, two.far())
        )
        dests = block_rows // dest_rows
        shaped = terms.T.astype(jnp.bfloat16).reshape(dests, dest_rows, width)
        for k in range(copies):
            held[pl.ds(index * dests, dests), k] = shaped
        if first is True:
            out.start()
        add_to(near_sum, jnp.dot(scaled, query_rows, preferred_element_type=jnp.float32), first)
        add_to(near2_sum, jnp.dot(scaled2, query_rows, preferred_element_type=jnp.float32), first)
        row = lax.broadcasted_iota(jnp.int32, loss_ref.shape, 0)
        add_to(loss_ref, jnp.where(row == 0, one.loss, two.loss), first)

    in_blocks(row_count, body)
    if row_count != math.gcd(row_count, ROW_BLOCK):
        out.start()
    out.wait()


def rest_body(
    query_len, page_len, limits_ref, rows_ref, near_ref, far_ref, near2_ref, far2_ref, sign_ref,
    sum_ref, sum2_ref, loss_in, near_out, sent_ref, loss_out, near_sum, near2_sum, loss_sum,
):
    row_count, width = rows_ref.shape
    tokens = near_ref.shape[0]
    scale = width ** (-0.5)

    def body(index, block_rows, first):
        offset = pl.multiple_of(index * block_rows, block_rows)
        query_rows = rows_ref[pl.ds(offset, block_rows), :]
        one, two = (
            Page(
                query_len, page_len, query_rows, a[...], b[...], limits_ref[2 * k], limits_ref[2 * k + 1],
                sign_ref[k : k + 1, pl.ds(offset, block_rows)],
            )
            for k, (a, b) in enumerate(((near_ref, far_ref), (near2_ref, far2_ref)))
        )
        add_to(near_sum, jnp.dot(one.near(), query_rows, preferred_element_type=jnp.float32), first)
        add_to(near2_sum, jnp.dot(two.near(), query_rows, preferred_element_type=jnp.float32), first)
        row = lax.broadcasted_iota(jnp.int32, loss_sum.shape, 0)
        add_to(loss_sum, jnp.where(row == 0, one.loss, two.loss), first)

    in_blocks(row_count, body)
    near_out[...] = (near_sum[...] + sum_ref[...]) * scale
    sent_ref[pl.ds(0, tokens), :] = ((near2_sum[...] + sum2_ref[...]) * scale).astype(jnp.bfloat16)
    losses = loss_in[...] + loss_sum[...]
    loss_out[...] = losses
    sent_ref[pl.ds(tokens, TAIL), :] = loss_parts(jnp.max(losses[1:2]))


def last_body(near_ref, loss_ref, got_ref, grad_ref, total_ref):
    tokens = near_ref.shape[0]
    grad_ref[0] = near_ref[...] + got_ref[pl.ds(0, tokens), :].astype(jnp.float32)
    total_ref[0] = jnp.max(loss_ref[0:1, :]) + loss_of(got_ref[pl.ds(tokens, TAIL), :])


def device_step(queries, pages, pad_counts, labels):
    query_count, query_len, width = queries.shape
    _, tokens, _ = pages.shape
    owners = lax.axis_size("pages")
    shares = lax.axis_size("tok")
    if shares != 2 or query_count % shares or owners % 2:
        raise ValueError("unsupported split")
    share = lax.axis_index("tok")
    side = lax.axis_index("pages") % 2
    page_len = tokens * shares
    picked = query_count // shares
    dest_rows = picked * query_len
    chips = owners // 2
    swap = [(0, 1), (1, 0)]
    partner = [(i, i ^ 1) for i in range(owners)]
    turn = chips // 2
    order = [(j + turn) % chips for j in range(chips)]
    same_side = [[2 * j + c for j in order] for c in range(2)]
    same_side_all = [
        [(2 * j + c) * shares + k for j in order for k in range(shares)] for c in range(2)
    ]
    vmem = pl.BlockSpec(memory_space=pltpu.VMEM)
    smem = pl.BlockSpec(memory_space=pltpu.SMEM)
    anywhere = pl.BlockSpec(memory_space=pl.ANY)
    params = pltpu.CompilerParams(vmem_limit_bytes=VMEM_BYTES)

    asked = pl.pallas_call(
        ask_body,
        out_shape=jax.ShapeDtypeStruct((chips, query_count, query_len, width), queries.dtype),
        in_specs=[anywhere],
        out_specs=anywhere,
        scratch_shapes=[pltpu.SemaphoreType.DMA((chips,))],
        compiler_params=params,
        name="ask_copies",
    )(queries)
    gathered = lax.all_to_all(
        asked.reshape(chips, query_count * query_len, width),
        "pages", 0, 0, tiled=True, axis_index_groups=same_side,
    ).reshape(chips, shares, dest_rows, width)

    near = pages[0]
    far = lax.ppermute(near, "tok", swap)
    near2 = lax.ppermute(near, "pages", partner)
    far2 = lax.ppermute(far, "pages", partner)
    facts = jnp.concatenate([labels[:, 0], pad_counts])
    facts2 = lax.ppermute(facts, "pages", partner)
    both = jnp.stack([facts, facts2])
    usable = page_len - both[:, -1:]
    limits = jnp.concatenate([usable - share * tokens, usable - (1 - share) * tokens], axis=1).reshape(4)
    label = jnp.roll(both[:, :-1].reshape(2, chips, 2, shares, picked), -turn, axis=1)
    label = 2.0 * lax.dynamic_index_in_dim(label, side, 2, False).astype(jnp.float32) - 1.0

    def of_share(index):
        rows = lax.dynamic_index_in_dim(gathered, index, 1, False).reshape(row_count, width)
        sign = lax.dynamic_index_in_dim(label, index, 2, False).reshape(2, chips * picked)
        return rows, jnp.repeat(sign, query_len, axis=1)

    row_count = chips * dest_rows
    rows, sign = of_share(share)
    rows_b, sign_b = of_share(1 - share)
    half = jax.ShapeDtypeStruct((tokens, width), jnp.float32)
    lane_row = jax.ShapeDtypeStruct((8, LANES), jnp.float32)
    blocks, near_sum, near2_sum, loss = pl.pallas_call(
        functools.partial(step_body, query_len, page_len),
        out_shape=(
            jax.ShapeDtypeStruct((chips, shares, dest_rows, width), jnp.bfloat16), half, half, lane_row,
        ),
        in_specs=[smem, vmem, vmem, vmem, vmem, vmem, vmem],
        out_specs=(anywhere, vmem, vmem, vmem),
        scratch_shapes=[
            pltpu.VMEM((chips, shares, dest_rows, width), jnp.bfloat16),
            pltpu.SemaphoreType.DMA,
        ],
        cost_estimate=pl.CostEstimate(
            flops=10 * row_count * page_len * width,
            transcendentals=2 * row_count * page_len,
            bytes_accessed=6 * row_count * width + 20 * tokens * width,
        ),
        compiler_params=params,
        name="page_step",
    )(limits, rows, near, far, near2, far2, sign)

    partials = lax.all_to_all(
        blocks.reshape(chips * shares, dest_rows, width),
        ("pages", "tok"), 0, 0, tiled=True, axis_index_groups=same_side_all,
    )
    near_sum, sent, loss = pl.pallas_call(
        functools.partial(rest_body, query_len, page_len),
        out_shape=(half, jax.ShapeDtypeStruct((tokens + TAIL, width), jnp.bfloat16), lane_row),
        in_specs=[smem] + [vmem] * 9,
        out_specs=(vmem,) * 3,
        scratch_shapes=[pltpu.VMEM((tokens, width), jnp.float32)] * 2 + [pltpu.VMEM((8, LANES), jnp.float32)],
        cost_estimate=pl.CostEstimate(
            flops=6 * row_count * page_len * width,
            transcendentals=2 * row_count * page_len,
            bytes_accessed=2 * row_count * width + 20 * tokens * width,
        ),
        compiler_params=params,
        name="page_rest",
    )(limits, rows_b, near, far, near2, far2, sign_b, near_sum, near2_sum, loss)
    got = lax.ppermute(sent, "pages", partner)
    page_grad, page_loss = pl.pallas_call(
        last_body,
        out_shape=(
            jax.ShapeDtypeStruct((1, tokens, width), jnp.float32),
            jax.ShapeDtypeStruct((1,), jnp.float32),
        ),
        in_specs=[vmem, vmem, vmem],
        out_specs=(vmem, smem),
        cost_estimate=pl.CostEstimate(flops=2 * tokens * width, transcendentals=0, bytes_accessed=12 * tokens * width),
        compiler_params=params,
        name="page_out",
    )(near_sum, loss, got)
    summed = jnp.sum(
        partials.reshape(chips, shares, dest_rows, width).astype(jnp.float32), axis=0
    ) * (width ** (-0.5))
    query_grad = summed.reshape(query_count, query_len, width)
    return query_grad, page_grad, page_loss


def solution(mesh):
    return jax.shard_map(
        device_step,
        mesh=mesh,
        in_specs=(P("pages", None, None), P("pages", "tok", None), P("pages"), P(None, "pages")),
        out_specs=(P("pages", None, None), P("pages", "tok", None), P("pages")),
        check_vma=False,
    )
```

time: 40.1 us -> 32.9 us (0.82)
  waiting for transfers between devices: 16.9 us -> 6.51 us
  Pallas kernels: 4.55 us -> 6.3 us
  local copies, waits for them, and re-layouts: 1.64 us -> 2.96 us
    all_to_all x1, waiting for transfers between devices: 7.69 us -> 1.16 us  [device_step(): lax.all_to_all(blocks.reshape(chips * shares, dest_rows, width), ('pages'...]
    ppermute x1 -> x0, waiting for transfers between devices: 3.3 us -> none  [device_step(): got2 = lax.ppermute(merged, 'tok', swap)]
    all_to_all x1, waiting for transfers between devices: 5.95 us -> 3.99 us  [device_step(): lax.all_to_all(asked.reshape(chips, query_count * query_len, width), 'pag...]
    pallas_call x2 -> x3, Pallas kernels: 3.74 us -> 5.56 us  [the longest x1 2.81 us: device_step(): pl.pallas_call(functools.partial(step_body, query_len, page_len), out_sha...]
    unnamed x6, local copies, waits for them, and re-layouts: 0.66 us -> 2.24 us
    ppermute x1, waiting for transfers between devices: 0.01 us -> 1.34 us  [device_step(): got = lax.ppermute(sent, 'pages', partner)]
    ppermute x1 -> x0, starting transfers between devices: 1.16 us -> none  [device_step(): got2 = lax.ppermute(merged, 'tok', swap)]
    all_to_all x1, starting transfers between devices: 3.51 us -> 4.23 us  [device_step(): lax.all_to_all(blocks.reshape(chips * shares, dest_rows, width), ('pages'...]
  transfers between devices with their start and end apart: 8 -> 7, of which waited for: 3 -> 3; matrix products, arithmetic and copies ran while one was open for 5% -> 3% of each run, Pallas kernels for 0% -> 11%
where the time goes in v3:
time: 32.9 us; the launch traced here: 32.5 us
  starting transfers between devices  14.3 us (43%)
  waiting for transfers between devices  6.51 us (20%)
  Pallas kernels  6.3 us (19%)
  local copies, waits for them, and re-layouts  2.96 us (9%)
  between operations  1.4 us (4%)
  other arithmetic  1.03 us (3%)
    all_to_all x1, starting transfers between devices, device_step(): lax.all_to_all(asked.reshape(chips, query_count * query_len, width), 'pag...  6.38 us
    all_to_all x1, starting transfers between devices, device_step(): lax.all_to_all(blocks.reshape(chips * shares, dest_rows, width), ('pages'...  4.23 us
    all_to_all x1, waiting for transfers between devices, device_step(): lax.all_to_all(asked.reshape(chips, query_count * query_len, width), 'pag...  3.99 us
    ppermute x1, starting transfers between devices, device_step(): far = lax.ppermute(near, 'tok', swap)  3.06 us
    pallas_call x1, Pallas kernels, device_step(): pl.pallas_call(functools.partial(step_body, query_len, page_len), out_sha...  2.81 us
    unnamed x6, local copies, waits for them, and re-layouts  2.24 us
    pallas_call x1, Pallas kernels, device_step(): pl.pallas_call(functools.partial(rest_body, query_len, page_len), out_sha...  2.04 us
    ppermute x1, waiting for transfers between devices, device_step(): got = lax.ppermute(sent, 'pages', partner)  1.34 us
  transfers between devices with their start and end apart: 7, of which 3 were waited for; matrix products, arithmetic and copies ran while one was open for 3% of the time, Pallas kernels for 11%

profile of v3, /device:TPU:0, one launch (start us, length us, event | category | flops | bytes accessed | tf_op | source)
XLA Modules:
  0.0 32.5 jit_solution(15189670465259824592)
XLA Ops:
  0.6 3.1 %collective-permute-start.1 = (bf16[512,128]{1,0:T(8,128)(2,1)}, bf16[512,128]{1,0:T(8,128)(2,1)S(1)}, u32[]{:S(2)}, u32[]{:S(2)}) collective-permute-start(bf16[512,128]{1,0:T(8,128)(2,1)} %bitcast.16), channel_id=1, source_target_pairs={{0,1},{1,0},{2,3},{3,2},{4,5},{5,4},{6,7},{7,6},{8,9},{9,8},{10,11... | collective-permute-start | bytes 393224 | tf_op jit(solution)/shard_map/ppermute | solution.py:245
  3.7 0.0 collective-permute-start.2
  4.3 0.0 copy-start.2
  4.4 0.6 %copy-done.2 = s32[32,1]{0,1:T(1,128)S(1)} copy-done((s32[32,1]{0,1:T(1,128)S(1)}, s32[32,1]{0,1:T(1,128)}, u32[]{:S(2)}) %copy-start.2) | copy-done | bytes 152
  5.0 0.1 pad_add_fusion.2
  5.1 0.5 %collective-permute-start = (s32[33]{0:T(128)S(1)}, s32[33]{0:T(128)S(1)}, u32[]{:S(2)}, u32[]{:S(2)}) collective-permute-start(s32[33]{0:T(128)S(1)} %pad_add_fusion.2), channel_id=1, source_target_pairs={{0,2},{2,0},{4,6},{6,4},{8,10},{10,8},{12,14},{14,12},{16,18},{18,... | collective-permute-start | bytes 404 | tf_op jit(solution)/shard_map/ppermute | solution.py:249
  5.6 0.0 copy-start.1
  5.6 0.7 %copy-done.1 = bf16[2,32,128]{2,1,0:T(8,128)(2,1)S(1)} copy-done((bf16[2,32,128]{2,1,0:T(8,128)(2,1)S(1)}, bf16[2,32,128]{2,1,0:T(8,128)(2,1)}, u32[]{:S(2)}) %copy-start.1) | copy-done | bytes 16408
  6.3 0.7 %ask_copies.1 = bf16[8,2,32,128]{3,2,1,0:T(8,128)(2,1)} custom-call(bf16[2,32,128]{2,1,0:T(8,128)(2,1)S(1)} %copy-done.1), custom_call_target="tpu_custom_call" | custom-call | tf_op jit(solution)/shard_map/ask_copies/pallas_call | solution.py:230
  7.0 6.4 %all-to-all-start = ((bf16[8,64,128]{2,1,0:T(8,128)(2,1)}), bf16[8,64,128]{2,1,0:T(8,128)(2,1)S(1)}, u32[]{:S(2)}, u32[]{:S(2)}) async-start(bf16[8,64,128]{2,1,0:T(8,128)(2,1)} %bitcast.3), calls=%async_computation | async-start | bytes 262144 | tf_op jit(solution)/shard_map/all_to_all | solution.py:239
  13.4 0.1 fusion.7
  13.5 0.0 collective-permute-done
  13.5 0.1 reshape.79
  13.6 0.1 copy.8
  13.7 0.1 copy.7
  13.8 0.1 fusion.5
  13.9 0.1 fusion.3
  14.0 0.0 collective-permute-done.1.far_ref
  14.0 0.1 collective-permute-start.3
  14.1 0.1 pad_add_fusion.1
  14.2 0.1 reshape.75.limits_ref
  14.2 0.1 broadcast_in_dim.6
  14.3 0.1 reshape.81.sign_ref
  14.4 4.0 %all-to-all-done = bf16[8,64,128]{2,1,0:T(8,128)(2,1)S(1)} async-done(((bf16[8,64,128]{2,1,0:T(8,128)(2,1)}), bf16[8,64,128]{2,1,0:T(8,128)(2,1)S(1)}, u32[]{:S(2)}, u32[]{:S(2)}) %all-to-all-start) | async-done | bytes 131104 | tf_op jit(solution)/shard_map/all_to_all | solution.py:239
  18.4 0.0 copy-start
  18.4 0.0 collective-permute-done.2.near2_ref
  18.4 0.0 collective-permute-done.3.far2_ref
  18.4 0.9 %copy-done = bf16[1,512,128]{2,1,0:T(8,128)(2,1)S(1)} copy-done((bf16[1,512,128]{2,1,0:T(8,128)(2,1)S(1)}, bf16[1,512,128]{2,1,0:T(8,128)(2,1)}, u32[]{:S(2)}) %copy-start) | copy-done | bytes 131096
  19.3 2.8 %page_step.1 = (bf16[8,2,32,128]{3,2,1,0:T(8,128)(2,1)}, f32[512,128]{1,0:T(8,128)S(1)}, f32[512,128]{1,0:T(8,128)S(1)}, f32[8,128]{1,0:T(8,128)S(1)}) custom-call(s32[4]{0:T(128)S(1)} %reshape.75.limits_ref, bf16[256,128]{1,0:T(8,128)(2,1)S(1)} %bitcast.20, bf16[512,128]{1,0:T(8,128)(2,1)S(1)} %bitcast.18, ...), custom_call_target="tpu_custom_call" | custom-call | flops 335544320 | bytes 1507328 | tf_op jit(solution)/shard_map/page_step/pallas_call | solution.py:266
  22.1 4.2 %all-to-all-start.1 = ((bf16[16,32,128]{2,1,0:T(8,128)(2,1)}), bf16[16,32,128]{2,1,0:T(8,128)(2,1)S(1)}, u32[]{:S(2)}, u32[]{:S(2)}) async-start(bf16[16,32,128]{2,1,0:T(8,128)(2,1)} %bitcast.8), calls=%async_computation.1 | async-start | bytes 262144 | tf_op jit(solution)/shard_map/all_to_all | solution.py:286
  26.3 0.1 broadcast_in_dim.7
  26.4 0.1 reshape.85.sign_ref
  26.5 2.0 %page_rest.1 = (f32[512,128]{1,0:T(8,128)S(1)}, bf16[528,128]{1,0:T(8,128)(2,1)S(1)}, f32[8,128]{1,0:T(8,128)S(1)}) custom-call(s32[4]{0:T(128)S(1)} %reshape.75.limits_ref, bf16[256,128]{1,0:T(8,128)(2,1)S(1)} %bitcast.15, bf16[512,128]{1,0:T(8,128)(2,1)S(1)} %bitcast.19, bf16[512,128]{1,0:T(8,128)(2,1)S(1)} %collective-permute-done.1.far_ref, ...), custom_call_target="tpu_custom_call" | custom-call | flops 201326592 | bytes 1376256 | tf_op jit(solution)/shard_map/page_rest/pallas_call | solution.py:290
  28.5 0.1 collective-permute-start.4
  28.6 1.3 %collective-permute-done.4.got_ref = bf16[528,128]{1,0:T(8,128)(2,1)S(1)} collective-permute-done((bf16[528,128]{1,0:T(8,128)(2,1)S(1)}, bf16[528,128]{1,0:T(8,128)(2,1)S(1)}, u32[]{:S(2)}, u32[]{:S(2)}) %collective-permute-start.4) | collective-permute-done | bytes 135200 | tf_op jit(solution)/shard_map/ppermute | solution.py:304
  30.0 0.7 %page_out.1 = (f32[1,512,128]{2,1,0:T(8,128)}, f32[1]{0:T(128)}) custom-call(f32[512,128]{1,0:T(8,128)S(1)} %get-tuple-element.16.near_ref, f32[8,128]{1,0:T(8,128)S(1)} %get-tuple-element.17.loss_ref, bf16[528,128]{1,0:T(8,128)(2,1)S(1)} %collective-permute-done.4.got_ref), custom_call_target="tpu_custom_call" | custom-call | flops 131072 | bytes 786432 | tf_op jit(solution)/shard_map/page_out/pallas_call | solution.py:305
  30.7 1.2 %all-to-all-done.1 = bf16[16,32,128]{2,1,0:T(8,128)(2,1)S(1)} async-done(((bf16[16,32,128]{2,1,0:T(8,128)(2,1)}), bf16[16,32,128]{2,1,0:T(8,128)(2,1)S(1)}, u32[]{:S(2)}, u32[]{:S(2)}) %all-to-all-start.1) | async-done | bytes 131104 | tf_op jit(solution)/shard_map/all_to_all | solution.py:286
  31.9 0.6 %broadcast_multiply_fusion = f32[2,32,128]{2,1,0:T(8,128)} fusion(f32[2,32,128]{2,1,0:T(8,128)S(1)} %convert_reduce_fusion), kind=kLoop, calls=%fused_computation.1 | loop fusion | flops 8192 | bytes 65536 | tf_op jit(solution)/shard_map/mul | solution.py:317
  (5 shorter events, 0.1 us)
Async XLA Ops:
  0.6 13.4 %collective-permute-start.1 = (bf16[512,128]{1,0:T(8,128)(2,1)}, bf16[512,128]{1,0:T(8,128)(2,1)S(1)}, u32[]{:S(2)}, u32[]{:S(2)}) collective-permute-start(bf16[512,128]{1,0:T(8,128)(2,1)} %bitcast.16), channel_id=1, source_target_pairs={{0,1},{1,0},{2,3},{3,2},{4,5},{5,4},{6,7},{7,6},{8,9},{9,8},{10,11... | collective-permute-start | bytes 393224 | tf_op jit(solution)/shard_map/ppermute | solution.py:245
  3.7 14.7 %collective-permute-start.2 = (bf16[512,128]{1,0:T(8,128)(2,1)}, bf16[512,128]{1,0:T(8,128)(2,1)S(1)}, u32[]{:S(2)}, u32[]{:S(2)}) collective-permute-start(bf16[512,128]{1,0:T(8,128)(2,1)} %bitcast.17), channel_id=1, source_target_pairs={{0,2},{2,0},{4,6},{6,4},{8,10},{10,8},{12,14},{14,12},{16,18},{18,... | collective-permute-start | bytes 393224 | tf_op jit(solution)/shard_map/ppermute | solution.py:246
  4.3 0.7 %copy-start.2 = (s32[32,1]{0,1:T(1,128)S(1)}, s32[32,1]{0,1:T(1,128)}, u32[]{:S(2)}) copy-start(s32[32,1]{0,1:T(1,128)} %param.7) | copy-start | bytes 388
  5.1 8.4 %collective-permute-start = (s32[33]{0:T(128)S(1)}, s32[33]{0:T(128)S(1)}, u32[]{:S(2)}, u32[]{:S(2)}) collective-permute-start(s32[33]{0:T(128)S(1)} %pad_add_fusion.2), channel_id=1, source_target_pairs={{0,2},{2,0},{4,6},{6,4},{8,10},{10,8},{12,14},{14,12},{16,18},{18,... | collective-permute-start | bytes 404 | tf_op jit(solution)/shard_map/ppermute | solution.py:249
  5.6 0.7 %copy-start.1 = (bf16[2,32,128]{2,1,0:T(8,128)(2,1)S(1)}, bf16[2,32,128]{2,1,0:T(8,128)(2,1)}, u32[]{:S(2)}) copy-start(bf16[2,32,128]{2,1,0:T(8,128)(2,1)} %queries_ref.1) | copy-start | bytes 49156
  7.0 11.4 %all-to-all-start = ((bf16[8,64,128]{2,1,0:T(8,128)(2,1)}), bf16[8,64,128]{2,1,0:T(8,128)(2,1)S(1)}, u32[]{:S(2)}, u32[]{:S(2)}) async-start(bf16[8,64,128]{2,1,0:T(8,128)(2,1)} %bitcast.3), calls=%async_computation | async-start | bytes 262144 | tf_op jit(solution)/shard_map/all_to_all | solution.py:239
  14.0 4.4 %collective-permute-start.3 = (bf16[512,128]{1,0:T(8,128)(2,1)S(1)}, bf16[512,128]{1,0:T(8,128)(2,1)S(1)}, u32[]{:S(2)}, u32[]{:S(2)}) collective-permute-start(bf16[512,128]{1,0:T(8,128)(2,1)S(1)} %collective-permute-done.1.far_ref), channel_id=1, source_target_pairs={{0,2},{2,0},{4,6},{6,4},{8,10},{10,8},{12,14},{14,12},{16,18},{18,... | collective-permute-start | bytes 393224 | tf_op jit(solution)/shard_map/ppermute | solution.py:247
  18.4 0.9 %copy-start = (bf16[1,512,128]{2,1,0:T(8,128)(2,1)S(1)}, bf16[1,512,128]{2,1,0:T(8,128)(2,1)}, u32[]{:S(2)}) copy-start(bf16[1,512,128]{2,1,0:T(8,128)(2,1)} %param.5) | copy-start | bytes 393220
  22.1 9.8 %all-to-all-start.1 = ((bf16[16,32,128]{2,1,0:T(8,128)(2,1)}), bf16[16,32,128]{2,1,0:T(8,128)(2,1)S(1)}, u32[]{:S(2)}, u32[]{:S(2)}) async-start(bf16[16,32,128]{2,1,0:T(8,128)(2,1)} %bitcast.8), calls=%async_computation.1 | async-start | bytes 262144 | tf_op jit(solution)/shard_map/all_to_all | solution.py:286
  28.5 1.4 %collective-permute-start.4 = (bf16[528,128]{1,0:T(8,128)(2,1)S(1)}, bf16[528,128]{1,0:T(8,128)(2,1)S(1)}, u32[]{:S(2)}, u32[]{:S(2)}) collective-permute-start(bf16[528,128]{1,0:T(8,128)(2,1)S(1)} %get-tuple-element.18), channel_id=1, source_target_pairs={{0,2},{2,0},{4,6},{6,4},{8,10},{10,8},{12,14},{14,12},{16,18},{18,... | collective-permute-start | bytes 405512 | tf_op jit(solution)/shard_map/ppermute | solution.py:304

commit v4 on v3

--- a/solution.py
+++ b/solution.py
@@ -16,6 +16,7 @@
 LANES = 128
 ROW_BLOCK = 256
 TAIL = 16
+SHIFT = 1
 VMEM_BYTES = 24 * 2**20
 
 
@@ -149,8 +150,10 @@
         )
         dests = block_rows // dest_rows
         shaped = terms.T.astype(jnp.bfloat16).reshape(dests, dest_rows, width)
-        for k in range(copies):
-            held[pl.ds(index * dests, dests), k] = shaped
+        for d in range(dests):
+            place = lax.rem(index * dests + d + held.shape[0] - SHIFT, held.shape[0])
+            for k in range(copies):
+                held[place, k] = shaped[d]
         if first is True:
             out.start()
         add_to(near_sum, jnp.dot(scaled, query_rows, preferred_element_type=jnp.float32), first)
@@ -219,8 +222,9 @@
     turn = chips // 2
     order = [(j + turn) % chips for j in range(chips)]
     same_side = [[2 * j + c for j in order] for c in range(2)]
+    later = order[SHIFT:] + order[:SHIFT]
     same_side_all = [
-        [(2 * j + c) * shares + k for j in order for k in range(shares)] for c in range(2)
+        [(2 * j + c) * shares + k for j in later for k in range(shares)] for c in range(2)
     ]
     vmem = pl.BlockSpec(memory_space=pltpu.VMEM)
     smem = pl.BlockSpec(memory_space=pltpu.SMEM)

time: 32.9 us -> 33 us (level)
  starting transfers between devices: 14.3 us -> 15.2 us
  waiting for transfers between devices: 6.51 us -> 5.69 us
    all_to_all x1, starting transfers between devices: 4.23 us -> 5.13 us  [device_step(): lax.all_to_all(blocks.reshape(chips * shares, dest_rows, width), ('pages'...]
    all_to_all x1, waiting for transfers between devices: 1.16 us -> 0.35 us  [device_step(): lax.all_to_all(blocks.reshape(chips * shares, dest_rows, width), ('pages'...]
where the time goes in v4:
time: 33 us; the launch traced here: 32.6 us
  starting transfers between devices  15.2 us (46%)
  Pallas kernels  6.3 us (19%)
  waiting for transfers between devices  5.69 us (17%)
  local copies, waits for them, and re-layouts  2.96 us (9%)
  between operations  1.4 us (4%)
  other arithmetic  1.03 us (3%)
    all_to_all x1, starting transfers between devices, device_step(): lax.all_to_all(asked.reshape(chips, query_count * query_len, width), 'pag...  6.38 us
    all_to_all x1, starting transfers between devices, device_step(): lax.all_to_all(blocks.reshape(chips * shares, dest_rows, width), ('pages'...  5.13 us
    all_to_all x1, waiting for transfers between devices, device_step(): lax.all_to_all(asked.reshape(chips, query_count * query_len, width), 'pag...  3.99 us
    ppermute x1, starting transfers between devices, device_step(): far = lax.ppermute(near, 'tok', swap)  3.06 us
    pallas_call x1, Pallas kernels, device_step(): pl.pallas_call(functools.partial(step_body, query_len, page_len), out_sha...  2.81 us
    unnamed x6, local copies, waits for them, and re-layouts  2.24 us
    pallas_call x1, Pallas kernels, device_step(): pl.pallas_call(functools.partial(rest_body, query_len, page_len), out_sha...  2.04 us
    ppermute x1, waiting for transfers between devices, device_step(): got = lax.ppermute(sent, 'pages', partner)  1.34 us
  transfers between devices with their start and end apart: 7, of which 3 were waited for; matrix products, arithmetic and copies ran while one was open for 3% of the time, Pallas kernels for 11%

profile of v4, /device:TPU:0, one launch (start us, length us, event | category | flops | bytes accessed | tf_op | source)
XLA Modules:
  0.0 32.6 jit_solution(17133054976511088583)
XLA Ops:
  0.6 3.1 %collective-permute-start.1 = (bf16[512,128]{1,0:T(8,128)(2,1)}, bf16[512,128]{1,0:T(8,128)(2,1)S(1)}, u32[]{:S(2)}, u32[]{:S(2)}) collective-permute-start(bf16[512,128]{1,0:T(8,128)(2,1)} %bitcast.16), channel_id=1, source_target_pairs={{0,1},{1,0},{2,3},{3,2},{4,5},{5,4},{6,7},{7,6},{8,9},{9,8},{10,11... | collective-permute-start | bytes 393224 | tf_op jit(solution)/shard_map/ppermute | solution.py:249
  3.7 0.0 collective-permute-start.2
  4.3 0.0 copy-start.2
  4.4 0.6 %copy-done.2 = s32[32,1]{0,1:T(1,128)S(1)} copy-done((s32[32,1]{0,1:T(1,128)S(1)}, s32[32,1]{0,1:T(1,128)}, u32[]{:S(2)}) %copy-start.2) | copy-done | bytes 152
  5.0 0.1 pad_add_fusion.2
  5.1 0.5 %collective-permute-start = (s32[33]{0:T(128)S(1)}, s32[33]{0:T(128)S(1)}, u32[]{:S(2)}, u32[]{:S(2)}) collective-permute-start(s32[33]{0:T(128)S(1)} %pad_add_fusion.2), channel_id=1, source_target_pairs={{0,2},{2,0},{4,6},{6,4},{8,10},{10,8},{12,14},{14,12},{16,18},{18,... | collective-permute-start | bytes 404 | tf_op jit(solution)/shard_map/ppermute | solution.py:253
  5.6 0.0 copy-start.1
  5.6 0.7 %copy-done.1 = bf16[2,32,128]{2,1,0:T(8,128)(2,1)S(1)} copy-done((bf16[2,32,128]{2,1,0:T(8,128)(2,1)S(1)}, bf16[2,32,128]{2,1,0:T(8,128)(2,1)}, u32[]{:S(2)}) %copy-start.1) | copy-done | bytes 16408
  6.3 0.7 %ask_copies.1 = bf16[8,2,32,128]{3,2,1,0:T(8,128)(2,1)} custom-call(bf16[2,32,128]{2,1,0:T(8,128)(2,1)S(1)} %copy-done.1), custom_call_target="tpu_custom_call" | custom-call | tf_op jit(solution)/shard_map/ask_copies/pallas_call | solution.py:234
  7.0 6.4 %all-to-all-start = ((bf16[8,64,128]{2,1,0:T(8,128)(2,1)}), bf16[8,64,128]{2,1,0:T(8,128)(2,1)S(1)}, u32[]{:S(2)}, u32[]{:S(2)}) async-start(bf16[8,64,128]{2,1,0:T(8,128)(2,1)} %bitcast.3), calls=%async_computation | async-start | bytes 262144 | tf_op jit(solution)/shard_map/all_to_all | solution.py:243
  13.4 0.1 fusion.7
  13.5 0.0 collective-permute-done
  13.5 0.1 reshape.79
  13.6 0.1 copy.8
  13.7 0.1 copy.7
  13.8 0.1 fusion.5
  13.9 0.1 fusion.3
  14.0 0.0 collective-permute-done.1.far_ref
  14.0 0.1 collective-permute-start.3
  14.1 0.1 pad_add_fusion.1
  14.2 0.1 reshape.75.limits_ref
  14.2 0.1 broadcast_in_dim.6
  14.3 0.1 reshape.81.sign_ref
  14.4 4.0 %all-to-all-done = bf16[8,64,128]{2,1,0:T(8,128)(2,1)S(1)} async-done(((bf16[8,64,128]{2,1,0:T(8,128)(2,1)}), bf16[8,64,128]{2,1,0:T(8,128)(2,1)S(1)}, u32[]{:S(2)}, u32[]{:S(2)}) %all-to-all-start) | async-done | bytes 131104 | tf_op jit(solution)/shard_map/all_to_all | solution.py:243
  18.4 0.0 copy-start
  18.4 0.0 collective-permute-done.2.near2_ref
  18.4 0.0 collective-permute-done.3.far2_ref
  18.4 0.9 %copy-done = bf16[1,512,128]{2,1,0:T(8,128)(2,1)S(1)} copy-done((bf16[1,512,128]{2,1,0:T(8,128)(2,1)S(1)}, bf16[1,512,128]{2,1,0:T(8,128)(2,1)}, u32[]{:S(2)}) %copy-start) | copy-done | bytes 131096
  19.3 2.8 %page_step.1 = (bf16[8,2,32,128]{3,2,1,0:T(8,128)(2,1)}, f32[512,128]{1,0:T(8,128)S(1)}, f32[512,128]{1,0:T(8,128)S(1)}, f32[8,128]{1,0:T(8,128)S(1)}) custom-call(s32[4]{0:T(128)S(1)} %reshape.75.limits_ref, bf16[256,128]{1,0:T(8,128)(2,1)S(1)} %bitcast.20, bf16[512,128]{1,0:T(8,128)(2,1)S(1)} %bitcast.18, ...), custom_call_target="tpu_custom_call" | custom-call | flops 335544320 | bytes 1507328 | tf_op jit(solution)/shard_map/page_step/pallas_call | solution.py:270
  22.1 5.1 %all-to-all-start.1 = ((bf16[16,32,128]{2,1,0:T(8,128)(2,1)}), bf16[16,32,128]{2,1,0:T(8,128)(2,1)S(1)}, u32[]{:S(2)}, u32[]{:S(2)}) async-start(bf16[16,32,128]{2,1,0:T(8,128)(2,1)} %bitcast.8), calls=%async_computation.1 | async-start | bytes 262144 | tf_op jit(solution)/shard_map/all_to_all | solution.py:290
  27.2 0.1 broadcast_in_dim.7
  27.3 0.1 reshape.85.sign_ref
  27.4 2.0 %page_rest.1 = (f32[512,128]{1,0:T(8,128)S(1)}, bf16[528,128]{1,0:T(8,128)(2,1)S(1)}, f32[8,128]{1,0:T(8,128)S(1)}) custom-call(s32[4]{0:T(128)S(1)} %reshape.75.limits_ref, bf16[256,128]{1,0:T(8,128)(2,1)S(1)} %bitcast.15, bf16[512,128]{1,0:T(8,128)(2,1)S(1)} %bitcast.19, bf16[512,128]{1,0:T(8,128)(2,1)S(1)} %collective-permute-done.1.far_ref, ...), custom_call_target="tpu_custom_call" | custom-call | flops 201326592 | bytes 1376256 | tf_op jit(solution)/shard_map/page_rest/pallas_call | solution.py:294
  29.4 0.1 collective-permute-start.4
  29.5 1.3 %collective-permute-done.4.got_ref = bf16[528,128]{1,0:T(8,128)(2,1)S(1)} collective-permute-done((bf16[528,128]{1,0:T(8,128)(2,1)S(1)}, bf16[528,128]{1,0:T(8,128)(2,1)S(1)}, u32[]{:S(2)}, u32[]{:S(2)}) %collective-permute-start.4) | collective-permute-done | bytes 135200 | tf_op jit(solution)/shard_map/ppermute | solution.py:308
  30.9 0.7 %page_out.1 = (f32[1,512,128]{2,1,0:T(8,128)}, f32[1]{0:T(128)}) custom-call(f32[512,128]{1,0:T(8,128)S(1)} %get-tuple-element.16.near_ref, f32[8,128]{1,0:T(8,128)S(1)} %get-tuple-element.17.loss_ref, bf16[528,128]{1,0:T(8,128)(2,1)S(1)} %collective-permute-done.4.got_ref), custom_call_target="tpu_custom_call" | custom-call | flops 131072 | bytes 786432 | tf_op jit(solution)/shard_map/page_out/pallas_call | solution.py:309
  31.6 0.3 %all-to-all-done.1 = bf16[16,32,128]{2,1,0:T(8,128)(2,1)S(1)} async-done(((bf16[16,32,128]{2,1,0:T(8,128)(2,1)}), bf16[16,32,128]{2,1,0:T(8,128)(2,1)S(1)}, u32[]{:S(2)}, u32[]{:S(2)}) %all-to-all-start.1) | async-done | bytes 131104 | tf_op jit(solution)/shard_map/all_to_all | solution.py:290
  32.0 0.6 %broadcast_multiply_fusion = f32[2,32,128]{2,1,0:T(8,128)} fusion(f32[2,32,128]{2,1,0:T(8,128)S(1)} %convert_reduce_fusion), kind=kLoop, calls=%fused_computation.1 | loop fusion | flops 8192 | bytes 65536 | tf_op jit(solution)/shard_map/mul | solution.py:321
  (5 shorter events, 0.1 us)
Async XLA Ops:
  0.6 13.4 %collective-permute-start.1 = (bf16[512,128]{1,0:T(8,128)(2,1)}, bf16[512,128]{1,0:T(8,128)(2,1)S(1)}, u32[]{:S(2)}, u32[]{:S(2)}) collective-permute-start(bf16[512,128]{1,0:T(8,128)(2,1)} %bitcast.16), channel_id=1, source_target_pairs={{0,1},{1,0},{2,3},{3,2},{4,5},{5,4},{6,7},{7,6},{8,9},{9,8},{10,11... | collective-permute-start | bytes 393224 | tf_op jit(solution)/shard_map/ppermute | solution.py:249
  3.7 14.7 %collective-permute-start.2 = (bf16[512,128]{1,0:T(8,128)(2,1)}, bf16[512,128]{1,0:T(8,128)(2,1)S(1)}, u32[]{:S(2)}, u32[]{:S(2)}) collective-permute-start(bf16[512,128]{1,0:T(8,128)(2,1)} %bitcast.17), channel_id=1, source_target_pairs={{0,2},{2,0},{4,6},{6,4},{8,10},{10,8},{12,14},{14,12},{16,18},{18,... | collective-permute-start | bytes 393224 | tf_op jit(solution)/shard_map/ppermute | solution.py:250
  4.3 0.7 %copy-start.2 = (s32[32,1]{0,1:T(1,128)S(1)}, s32[32,1]{0,1:T(1,128)}, u32[]{:S(2)}) copy-start(s32[32,1]{0,1:T(1,128)} %param.7) | copy-start | bytes 388
  5.1 8.4 %collective-permute-start = (s32[33]{0:T(128)S(1)}, s32[33]{0:T(128)S(1)}, u32[]{:S(2)}, u32[]{:S(2)}) collective-permute-start(s32[33]{0:T(128)S(1)} %pad_add_fusion.2), channel_id=1, source_target_pairs={{0,2},{2,0},{4,6},{6,4},{8,10},{10,8},{12,14},{14,12},{16,18},{18,... | collective-permute-start | bytes 404 | tf_op jit(solution)/shard_map/ppermute | solution.py:253
  5.6 0.7 %copy-start.1 = (bf16[2,32,128]{2,1,0:T(8,128)(2,1)S(1)}, bf16[2,32,128]{2,1,0:T(8,128)(2,1)}, u32[]{:S(2)}) copy-start(bf16[2,32,128]{2,1,0:T(8,128)(2,1)} %queries_ref.1) | copy-start | bytes 49156
  7.0 11.4 %all-to-all-start = ((bf16[8,64,128]{2,1,0:T(8,128)(2,1)}), bf16[8,64,128]{2,1,0:T(8,128)(2,1)S(1)}, u32[]{:S(2)}, u32[]{:S(2)}) async-start(bf16[8,64,128]{2,1,0:T(8,128)(2,1)} %bitcast.3), calls=%async_computation | async-start | bytes 262144 | tf_op jit(solution)/shard_map/all_to_all | solution.py:243
  14.0 4.4 %collective-permute-start.3 = (bf16[512,128]{1,0:T(8,128)(2,1)S(1)}, bf16[512,128]{1,0:T(8,128)(2,1)S(1)}, u32[]{:S(2)}, u32[]{:S(2)}) collective-permute-start(bf16[512,128]{1,0:T(8,128)(2,1)S(1)} %collective-permute-done.1.far_ref), channel_id=1, source_target_pairs={{0,2},{2,0},{4,6},{6,4},{8,10},{10,8},{12,14},{14,12},{16,18},{18,... | collective-permute-start | bytes 393224 | tf_op jit(solution)/shard_map/ppermute | solution.py:251
  18.4 0.9 %copy-start = (bf16[1,512,128]{2,1,0:T(8,128)(2,1)S(1)}, bf16[1,512,128]{2,1,0:T(8,128)(2,1)}, u32[]{:S(2)}) copy-start(bf16[1,512,128]{2,1,0:T(8,128)(2,1)} %param.5) | copy-start | bytes 393220
  22.1 9.8 %all-to-all-start.1 = ((bf16[16,32,128]{2,1,0:T(8,128)(2,1)}), bf16[16,32,128]{2,1,0:T(8,128)(2,1)S(1)}, u32[]{:S(2)}, u32[]{:S(2)}) async-start(bf16[16,32,128]{2,1,0:T(8,128)(2,1)} %bitcast.8), calls=%async_computation.1 | async-start | bytes 262144 | tf_op jit(solution)/shard_map/all_to_all | solution.py:290
  29.4 1.4 %collective-permute-start.4 = (bf16[528,128]{1,0:T(8,128)(2,1)S(1)}, bf16[528,128]{1,0:T(8,128)(2,1)S(1)}, u32[]{:S(2)}, u32[]{:S(2)}) collective-permute-start(bf16[528,128]{1,0:T(8,128)(2,1)S(1)} %get-tuple-element.18), channel_id=1, source_target_pairs={{0,2},{2,0},{4,6},{6,4},{8,10},{10,8},{12,14},{14,12},{16,18},{18,... | collective-permute-start | bytes 405512 | tf_op jit(solution)/shard_map/ppermute | solution.py:308

commit v5 on v4

--- a/solution.py
+++ b/solution.py
@@ -64,17 +64,19 @@
 
 
 class Page:
-    def __init__(self, query_len, page_len, query_rows, near, far, limit_near, limit_far, sign):
-        tokens, width = near.shape
+    def __init__(self, query_len, page_len, query_rows, near, far, bias_near, bias_far, sign):
+        _, width = near.shape
         block_rows = query_rows.shape[0]
         pieces = block_rows // LANES
         scale = width ** (-0.5)
         rate = scale * math.log2(math.e)
         gain = LOGIT_SPAN / query_len
         centre = query_len * (CENTRE_SHIFT + math.log(FILL_SHARE * page_len))
-        place = lax.broadcasted_iota(jnp.int32, (tokens, block_rows), 0)
-        raw_near = jnp.where(place < limit_near, over_features(near, query_rows), MASKED)
-        raw_far = jnp.where(place < limit_far, over_features(far, query_rows), MASKED)
+        lane = lax.broadcasted_iota(jnp.int32, (block_rows, LANES), 1)
+        one = jnp.where(lane == 0, 1.0, 0.0).astype(jnp.bfloat16)
+        wide_rows = jnp.concatenate([query_rows, one], axis=1)
+        raw_near = over_features(jnp.concatenate([near, bias_near], axis=1), wide_rows)
+        raw_far = over_features(jnp.concatenate([far, bias_far], axis=1), wide_rows)
         highest = jnp.maximum(
             jnp.max(raw_near, axis=0, keepdims=True), jnp.max(raw_far, axis=0, keepdims=True)
         )
@@ -101,8 +103,9 @@
     def near(self):
         return (self.exp_near * self.factor).astype(jnp.bfloat16)
 
-    def far(self):
-        return (self.exp_far * self.factor).astype(jnp.bfloat16)
+    def query_terms(self, near, far):
+        terms = over_tokens(near, self.exp_near.astype(jnp.bfloat16))
+        return (terms + over_tokens(far, self.exp_far.astype(jnp.bfloat16))) * self.factor
 
 
 def in_blocks(row_count, body):
@@ -125,8 +128,8 @@
 
 
 def step_body(
-    query_len, page_len, limits_ref, rows_ref, near_ref, far_ref, near2_ref, far2_ref, sign_ref,
-    blocks_ref, near_sum, near2_sum, loss_ref, held, sem,
+    query_len, page_len, bias_ref, rows_ref, near_ref, far_ref, near2_ref, far2_ref, sign_ref,
+    blocks_ref, sums_ref, loss_ref, held, kept, factors, sem,
 ):
     row_count, width = rows_ref.shape
     copies, dest_rows = held.shape[1:3]
@@ -138,28 +141,34 @@
         near, far, near2, far2 = near_ref[...], far_ref[...], near2_ref[...], far2_ref[...]
         one, two = (
             Page(
-                query_len, page_len, query_rows, a, b, limits_ref[2 * k], limits_ref[2 * k + 1],
+                query_len, page_len, query_rows, a, b, bias_ref[2 * k], bias_ref[2 * k + 1],
                 sign_ref[k : k + 1, pl.ds(offset, block_rows)],
             )
             for k, (a, b) in enumerate(((near, far), (near2, far2)))
         )
-        scaled, scaled2 = one.near(), two.near()
-        terms = (
-            over_tokens(near, scaled) + over_tokens(far, one.far())
-            + over_tokens(near2, scaled2) + over_tokens(far2, two.far())
-        )
+        terms = one.query_terms(near, far) + two.query_terms(near2, far2)
         dests = block_rows // dest_rows
         shaped = terms.T.astype(jnp.bfloat16).reshape(dests, dest_rows, width)
         for d in range(dests):
             place = lax.rem(index * dests + d + held.shape[0] - SHIFT, held.shape[0])
             for k in range(copies):
                 held[place, k] = shaped[d]
+        for k, page in enumerate((one, two)):
+            kept[k] = page.exp_near
+            factors[k] = page.factor
         if first is True:
             out.start()
-        add_to(near_sum, jnp.dot(scaled, query_rows, preferred_element_type=jnp.float32), first)
-        add_to(near2_sum, jnp.dot(scaled2, query_rows, preferred_element_type=jnp.float32), first)
         row = lax.broadcasted_iota(jnp.int32, loss_ref.shape, 0)
         add_to(loss_ref, jnp.where(row == 0, one.loss, two.loss), first)
+
+        @pl.loop(0, 2)
+        def _(page):
+            scaled = (kept[page] * factors[page]).astype(jnp.bfloat16)
+            add_to(
+                sums_ref.at[page],
+                jnp.dot(scaled, rows_ref[pl.ds(offset, block_rows), :], preferred_element_type=jnp.float32),
+                first,
+            )
 
     in_blocks(row_count, body)
     if row_count != math.gcd(row_count, ROW_BLOCK):
@@ -168,8 +177,8 @@
 
 
 def rest_body(
-    query_len, page_len, limits_ref, rows_ref, near_ref, far_ref, near2_ref, far2_ref, sign_ref,
-    sum_ref, sum2_ref, loss_in, near_out, sent_ref, loss_out, near_sum, near2_sum, loss_sum,
+    query_len, page_len, bias_ref, rows_ref, near_ref, far_ref, near2_ref, far2_ref, sign_ref,
+    sums_ref, loss_in, near_out, sent_ref, loss_out, near_sum, near2_sum, loss_sum,
 ):
     row_count, width = rows_ref.shape
     tokens = near_ref.shape[0]
@@ -180,7 +189,7 @@
         query_rows = rows_ref[pl.ds(offset, block_rows), :]
         one, two = (
             Page(
-                query_len, page_len, query_rows, a[...], b[...], limits_ref[2 * k], limits_ref[2 * k + 1],
+                query_len, page_len, query_rows, a[...], b[...], bias_ref[2 * k], bias_ref[2 * k + 1],
                 sign_ref[k : k + 1, pl.ds(offset, block_rows)],
             )
             for k, (a, b) in enumerate(((near_ref, far_ref), (near2_ref, far2_ref)))
@@ -191,11 +200,20 @@
         add_to(loss_sum, jnp.where(row == 0, one.loss, two.loss), first)
 
     in_blocks(row_count, body)
-    near_out[...] = (near_sum[...] + sum_ref[...]) * scale
-    sent_ref[pl.ds(0, tokens), :] = ((near2_sum[...] + sum2_ref[...]) * scale).astype(jnp.bfloat16)
+    near_out[...] = (near_sum[...] + sums_ref[0]) * scale
+    sent_ref[pl.ds(0, tokens), :] = ((near2_sum[...] + sums_ref[1]) * scale).astype(jnp.bfloat16)
     losses = loss_in[...] + loss_sum[...]
     loss_out[...] = losses
     sent_ref[pl.ds(tokens, TAIL), :] = loss_parts(jnp.max(losses[1:2]))
+
+
+def bias_body(limits_ref, bias_ref):
+    shape = bias_ref.shape[1:]
+    row = lax.broadcasted_iota(jnp.int32, shape, 0)
+    lane = lax.broadcasted_iota(jnp.int32, shape, 1)
+    for k in range(bias_ref.shape[0]):
+        padding = (row >= limits_ref[k]) & (lane == 0)
+        bias_ref[k] = jnp.where(padding, MASKED, 0.0).astype(jnp.bfloat16)
 
 
 def last_body(near_ref, loss_ref, got_ref, grad_ref, total_ref):
@@ -267,15 +285,29 @@
     rows_b, sign_b = of_share(1 - share)
     half = jax.ShapeDtypeStruct((tokens, width), jnp.float32)
     lane_row = jax.ShapeDtypeStruct((8, LANES), jnp.float32)
-    blocks, near_sum, near2_sum, loss = pl.pallas_call(
+    bias = pl.pallas_call(
+        bias_body,
+        out_shape=jax.ShapeDtypeStruct((4, tokens, LANES), jnp.bfloat16),
+        in_specs=[smem],
+        out_specs=vmem,
+        cost_estimate=pl.CostEstimate(flops=0, transcendentals=0, bytes_accessed=8 * tokens * width),
+        compiler_params=params,
+        name="page_bias",
+    )(limits)
+    block_rows = math.gcd(row_count, ROW_BLOCK)
+    blocks, sums, loss = pl.pallas_call(
         functools.partial(step_body, query_len, page_len),
         out_shape=(
-            jax.ShapeDtypeStruct((chips, shares, dest_rows, width), jnp.bfloat16), half, half, lane_row,
+            jax.ShapeDtypeStruct((chips, shares, dest_rows, width), jnp.bfloat16),
+            jax.ShapeDtypeStruct((2, tokens, width), jnp.float32),
+            lane_row,
         ),
-        in_specs=[smem, vmem, vmem, vmem, vmem, vmem, vmem],
-        out_specs=(anywhere, vmem, vmem, vmem),
+        in_specs=[vmem] * 7,
+        out_specs=(anywhere, vmem, vmem),
         scratch_shapes=[
             pltpu.VMEM((chips, shares, dest_rows, width), jnp.bfloat16),
+            pltpu.VMEM((2, tokens, block_rows), jnp.float32),
+            pltpu.VMEM((2, 1, block_rows), jnp.float32),
             pltpu.SemaphoreType.DMA,
         ],
         cost_estimate=pl.CostEstimate(
@@ -285,7 +317,7 @@
         ),
         compiler_params=params,
         name="page_step",
-    )(limits, rows, near, far, near2, far2, sign)
+    )(bias, rows, near, far, near2, far2, sign)
 
     partials = lax.all_to_all(
         blocks.reshape(chips * shares, dest_rows, width),
@@ -294,7 +326,7 @@
     near_sum, sent, loss = pl.pallas_call(
         functools.partial(rest_body, query_len, page_len),
         out_shape=(half, jax.ShapeDtypeStruct((tokens + TAIL, width), jnp.bfloat16), lane_row),
-        in_specs=[smem] + [vmem] * 9,
+        in_specs=[vmem] * 9,
         out_specs=(vmem,) * 3,
         scratch_shapes=[pltpu.VMEM((tokens, width), jnp.float32)] * 2 + [pltpu.VMEM((8, LANES), jnp.float32)],
         cost_estimate=pl.CostEstimate(
@@ -304,7 +336,7 @@
         ),
         compiler_params=params,
         name="page_rest",
-    )(limits, rows_b, near, far, near2, far2, sign_b, near_sum, near2_sum, loss)
+    )(bias, rows_b, near, far, near2, far2, sign_b, sums, loss)
     got = lax.ppermute(sent, "pages", partner)
     page_grad, page_loss = pl.pallas_call(
         last_body,

time: 33 us -> 32.3 us (0.979)
  Pallas kernels: 6.3 us -> 5.62 us
    pallas_call x1, Pallas kernels: 2.81 us -> 2.06 us  [device_step(): pl.pallas_call(functools.partial(step_body, query_len, page_len), out_sha...]
    all_to_all x1, waiting for transfers between devices: 3.99 us -> 3.34 us  [device_step(): lax.all_to_all(asked.reshape(chips, query_count * query_len, width), 'pag...]
    pallas_call x0 -> x1, Pallas kernels: none -> 0.64 us  [device_step(): pl.pallas_call(bias_body, out_shape=jax.ShapeDtypeStruct((4, tokens, LANE...]
    all_to_all x1, waiting for transfers between devices: 0.35 us -> 0.93 us  [device_step(): lax.all_to_all(blocks.reshape(chips * shares, dest_rows, width), ('pages'...]
    pallas_call x1, Pallas kernels: 2.04 us -> 1.46 us  [device_step(): pl.pallas_call(functools.partial(rest_body, query_len, page_len), out_sha...]
where the time goes in v5:
time: 32.3 us; the launch traced here: 31.8 us
  starting transfers between devices  15.2 us (47%)
  Pallas kernels  5.62 us (17%)
  waiting for transfers between devices  5.62 us (17%)
  local copies, waits for them, and re-layouts  2.96 us (9%)
  between operations  1.4 us (4%)
  other arithmetic  1.03 us (3%)
    all_to_all x1, starting transfers between devices, device_step(): lax.all_to_all(asked.reshape(chips, query_count * query_len, width), 'pag...  6.38 us
    all_to_all x1, starting transfers between devices, device_step(): lax.all_to_all(blocks.reshape(chips * shares, dest_rows, width), ('pages'...  5.13 us
    all_to_all x1, waiting for transfers between devices, device_step(): lax.all_to_all(asked.reshape(chips, query_count * query_len, width), 'pag...  3.34 us
    ppermute x1, starting transfers between devices, device_step(): far = lax.ppermute(near, 'tok', swap)  3.06 us
    unnamed x6, local copies, waits for them, and re-layouts  2.24 us
    pallas_call x1, Pallas kernels, device_step(): pl.pallas_call(functools.partial(step_body, query_len, page_len), out_sha...  2.06 us
    pallas_call x1, Pallas kernels, device_step(): pl.pallas_call(functools.partial(rest_body, query_len, page_len), out_sha...  1.46 us
    ppermute x1, waiting for transfers between devices, device_step(): got = lax.ppermute(sent, 'pages', partner)  1.34 us
  transfers between devices with their start and end apart: 7, of which 3 were waited for; matrix products, arithmetic and copies ran while one was open for 3% of the time, Pallas kernels for 11%

profile of v5, /device:TPU:0, one launch (start us, length us, event | category | flops | bytes accessed | tf_op | source)
XLA Modules:
  0.0 31.8 jit_solution(16048134737515249921)
XLA Ops:
  0.6 3.1 %collective-permute-start.1 = (bf16[512,128]{1,0:T(8,128)(2,1)}, bf16[512,128]{1,0:T(8,128)(2,1)S(1)}, u32[]{:S(2)}, u32[]{:S(2)}) collective-permute-start(bf16[512,128]{1,0:T(8,128)(2,1)} %bitcast.16), channel_id=1, source_target_pairs={{0,1},{1,0},{2,3},{3,2},{4,5},{5,4},{6,7},{7,6},{8,9},{9,8},{10,11... | collective-permute-start | bytes 393224 | tf_op jit(solution)/shard_map/ppermute | solution.py:267
  3.7 0.0 collective-permute-start.2
  4.3 0.0 copy-start.2
  4.4 0.6 %copy-done.2 = s32[32,1]{0,1:T(1,128)S(1)} copy-done((s32[32,1]{0,1:T(1,128)S(1)}, s32[32,1]{0,1:T(1,128)}, u32[]{:S(2)}) %copy-start.2) | copy-done | bytes 152
  5.0 0.1 pad_add_fusion.2
  5.1 0.5 %collective-permute-start = (s32[33]{0:T(128)S(1)}, s32[33]{0:T(128)S(1)}, u32[]{:S(2)}, u32[]{:S(2)}) collective-permute-start(s32[33]{0:T(128)S(1)} %pad_add_fusion.2), channel_id=1, source_target_pairs={{0,2},{2,0},{4,6},{6,4},{8,10},{10,8},{12,14},{14,12},{16,18},{18,... | collective-permute-start | bytes 404 | tf_op jit(solution)/shard_map/ppermute | solution.py:271
  5.6 0.0 copy-start.1
  5.6 0.7 %copy-done.1 = bf16[2,32,128]{2,1,0:T(8,128)(2,1)S(1)} copy-done((bf16[2,32,128]{2,1,0:T(8,128)(2,1)S(1)}, bf16[2,32,128]{2,1,0:T(8,128)(2,1)}, u32[]{:S(2)}) %copy-start.1) | copy-done | bytes 16408
  6.3 0.7 %ask_copies.1 = bf16[8,2,32,128]{3,2,1,0:T(8,128)(2,1)} custom-call(bf16[2,32,128]{2,1,0:T(8,128)(2,1)S(1)} %copy-done.1), custom_call_target="tpu_custom_call" | custom-call | tf_op jit(solution)/shard_map/ask_copies/pallas_call | solution.py:252
  7.0 6.4 %all-to-all-start = ((bf16[8,64,128]{2,1,0:T(8,128)(2,1)}), bf16[8,64,128]{2,1,0:T(8,128)(2,1)S(1)}, u32[]{:S(2)}, u32[]{:S(2)}) async-start(bf16[8,64,128]{2,1,0:T(8,128)(2,1)} %bitcast.3), calls=%async_computation | async-start | bytes 262144 | tf_op jit(solution)/shard_map/all_to_all | solution.py:261
  13.4 0.1 fusion.7
  13.5 0.0 collective-permute-done
  13.5 0.1 reshape.79
  13.6 0.1 copy.8
  13.7 0.1 copy.7
  13.8 0.1 fusion.5
  13.9 0.1 fusion.3
  14.0 0.0 collective-permute-done.1.far_ref
  14.0 0.1 collective-permute-start.3
  14.1 0.1 pad_add_fusion.1
  14.2 0.1 reshape.75.limits_ref
  14.2 0.6 %page_bias.1.bias_ref = bf16[4,512,128]{2,1,0:T(8,128)(2,1)S(1)} custom-call(s32[4]{0:T(128)S(1)} %reshape.75.limits_ref), custom_call_target="tpu_custom_call" | custom-call | bytes 524288 | tf_op jit(solution)/shard_map/page_bias/pallas_call | solution.py:288
  14.9 0.1 broadcast_in_dim.6
  15.0 0.1 reshape.81.sign_ref
  15.0 3.3 %all-to-all-done = bf16[8,64,128]{2,1,0:T(8,128)(2,1)S(1)} async-done(((bf16[8,64,128]{2,1,0:T(8,128)(2,1)}), bf16[8,64,128]{2,1,0:T(8,128)(2,1)S(1)}, u32[]{:S(2)}, u32[]{:S(2)}) %all-to-all-start) | async-done | bytes 131104 | tf_op jit(solution)/shard_map/all_to_all | solution.py:261
  18.4 0.0 copy-start
  18.4 0.0 collective-permute-done.2.near2_ref
  18.4 0.0 collective-permute-done.3.far2_ref
  18.4 0.9 %copy-done = bf16[1,512,128]{2,1,0:T(8,128)(2,1)S(1)} copy-done((bf16[1,512,128]{2,1,0:T(8,128)(2,1)S(1)}, bf16[1,512,128]{2,1,0:T(8,128)(2,1)}, u32[]{:S(2)}) %copy-start) | copy-done | bytes 131096
  19.3 2.1 %page_step.1 = (bf16[8,2,32,128]{3,2,1,0:T(8,128)(2,1)}, f32[2,512,128]{2,1,0:T(8,128)S(1)}, f32[8,128]{1,0:T(8,128)S(1)}) custom-call(bf16[4,512,128]{2,1,0:T(8,128)(2,1)S(1)} %page_bias.1.bias_ref, bf16[256,128]{1,0:T(8,128)(2,1)S(1)} %bitcast.20, bf16[512,128]{1,0:T(8,128)(2,1)S(1)} %bitcast.18, bf16[512,128]{1,0:T(8,128)(2,1)S(1)} %collective-permute-done.1.far_ref, ...), custom_call_target="tpu_custom_call" | custom-call | flops 335544320 | bytes 1507328 | tf_op jit(solution)/shard_map/page_step/pallas_call | solution.py:298
  21.4 5.1 %all-to-all-start.1 = ((bf16[16,32,128]{2,1,0:T(8,128)(2,1)}), bf16[16,32,128]{2,1,0:T(8,128)(2,1)S(1)}, u32[]{:S(2)}, u32[]{:S(2)}) async-start(bf16[16,32,128]{2,1,0:T(8,128)(2,1)} %bitcast.8), calls=%async_computation.1 | async-start | bytes 262144 | tf_op jit(solution)/shard_map/all_to_all | solution.py:322
  26.5 0.1 broadcast_in_dim.7
  26.6 0.1 reshape.85.sign_ref
  26.6 1.5 %page_rest.1 = (f32[512,128]{1,0:T(8,128)S(1)}, bf16[528,128]{1,0:T(8,128)(2,1)S(1)}, f32[8,128]{1,0:T(8,128)S(1)}) custom-call(bf16[4,512,128]{2,1,0:T(8,128)(2,1)S(1)} %page_bias.1.bias_ref, bf16[256,128]{1,0:T(8,128)(2,1)S(1)} %bitcast.15, bf16[512,128]{1,0:T(8,128)(2,1)S(1)} %bitcast.19, bf16[512,128]{1,0:T(8,128)(2,1)S(1)} %collective-permute-done.1.far_ref, ...), custom_call_target="tpu_custom_call" | custom-call | flops 201326592 | bytes 1376256 | tf_op jit(solution)/shard_map/page_rest/pallas_call | solution.py:326
  28.1 0.1 collective-permute-start.4
  28.2 1.3 %collective-permute-done.4.got_ref = bf16[528,128]{1,0:T(8,128)(2,1)S(1)} collective-permute-done((bf16[528,128]{1,0:T(8,128)(2,1)S(1)}, bf16[528,128]{1,0:T(8,128)(2,1)S(1)}, u32[]{:S(2)}, u32[]{:S(2)}) %collective-permute-start.4) | collective-permute-done | bytes 135200 | tf_op jit(solution)/shard_map/ppermute | solution.py:340
  29.5 0.7 %page_out.1 = (f32[1,512,128]{2,1,0:T(8,128)}, f32[1]{0:T(128)}) custom-call(f32[512,128]{1,0:T(8,128)S(1)} %get-tuple-element.14.near_ref, f32[8,128]{1,0:T(8,128)S(1)} %get-tuple-element.15.loss_ref, bf16[528,128]{1,0:T(8,128)(2,1)S(1)} %collective-permute-done.4.got_ref), custom_call_target="tpu_custom_call" | custom-call | flops 131072 | bytes 786432 | tf_op jit(solution)/shard_map/page_out/pallas_call | solution.py:341
  30.3 0.9 %all-to-all-done.1 = bf16[16,32,128]{2,1,0:T(8,128)(2,1)S(1)} async-done(((bf16[16,32,128]{2,1,0:T(8,128)(2,1)}), bf16[16,32,128]{2,1,0:T(8,128)(2,1)S(1)}, u32[]{:S(2)}, u32[]{:S(2)}) %all-to-all-start.1) | async-done | bytes 131104 | tf_op jit(solution)/shard_map/all_to_all | solution.py:322
  31.2 0.6 %broadcast_multiply_fusion = f32[2,32,128]{2,1,0:T(8,128)} fusion(f32[2,32,128]{2,1,0:T(8,128)S(1)} %convert_reduce_fusion), kind=kLoop, calls=%fused_computation.1 | loop fusion | flops 8192 | bytes 65536 | tf_op jit(solution)/shard_map/mul | solution.py:353
  (5 shorter events, 0.1 us)
Async XLA Ops:
  0.6 13.4 %collective-permute-start.1 = (bf16[512,128]{1,0:T(8,128)(2,1)}, bf16[512,128]{1,0:T(8,128)(2,1)S(1)}, u32[]{:S(2)}, u32[]{:S(2)}) collective-permute-start(bf16[512,128]{1,0:T(8,128)(2,1)} %bitcast.16), channel_id=1, source_target_pairs={{0,1},{1,0},{2,3},{3,2},{4,5},{5,4},{6,7},{7,6},{8,9},{9,8},{10,11... | collective-permute-start | bytes 393224 | tf_op jit(solution)/shard_map/ppermute | solution.py:267
  3.7 14.7 %collective-permute-start.2 = (bf16[512,128]{1,0:T(8,128)(2,1)}, bf16[512,128]{1,0:T(8,128)(2,1)S(1)}, u32[]{:S(2)}, u32[]{:S(2)}) collective-permute-start(bf16[512,128]{1,0:T(8,128)(2,1)} %bitcast.17), channel_id=1, source_target_pairs={{0,2},{2,0},{4,6},{6,4},{8,10},{10,8},{12,14},{14,12},{16,18},{18,... | collective-permute-start | bytes 393224 | tf_op jit(solution)/shard_map/ppermute | solution.py:268
  4.3 0.7 %copy-start.2 = (s32[32,1]{0,1:T(1,128)S(1)}, s32[32,1]{0,1:T(1,128)}, u32[]{:S(2)}) copy-start(s32[32,1]{0,1:T(1,128)} %param.7) | copy-start | bytes 388
  5.1 8.4 %collective-permute-start = (s32[33]{0:T(128)S(1)}, s32[33]{0:T(128)S(1)}, u32[]{:S(2)}, u32[]{:S(2)}) collective-permute-start(s32[33]{0:T(128)S(1)} %pad_add_fusion.2), channel_id=1, source_target_pairs={{0,2},{2,0},{4,6},{6,4},{8,10},{10,8},{12,14},{14,12},{16,18},{18,... | collective-permute-start | bytes 404 | tf_op jit(solution)/shard_map/ppermute | solution.py:271
  5.6 0.7 %copy-start.1 = (bf16[2,32,128]{2,1,0:T(8,128)(2,1)S(1)}, bf16[2,32,128]{2,1,0:T(8,128)(2,1)}, u32[]{:S(2)}) copy-start(bf16[2,32,128]{2,1,0:T(8,128)(2,1)} %queries_ref.1) | copy-start | bytes 49156
  7.0 11.4 %all-to-all-start = ((bf16[8,64,128]{2,1,0:T(8,128)(2,1)}), bf16[8,64,128]{2,1,0:T(8,128)(2,1)S(1)}, u32[]{:S(2)}, u32[]{:S(2)}) async-start(bf16[8,64,128]{2,1,0:T(8,128)(2,1)} %bitcast.3), calls=%async_computation | async-start | bytes 262144 | tf_op jit(solution)/shard_map/all_to_all | solution.py:261
  14.0 4.4 %collective-permute-start.3 = (bf16[512,128]{1,0:T(8,128)(2,1)S(1)}, bf16[512,128]{1,0:T(8,128)(2,1)S(1)}, u32[]{:S(2)}, u32[]{:S(2)}) collective-permute-start(bf16[512,128]{1,0:T(8,128)(2,1)S(1)} %collective-permute-done.1.far_ref), channel_id=1, source_target_pairs={{0,2},{2,0},{4,6},{6,4},{8,10},{10,8},{12,14},{14,12},{16,18},{18,... | collective-permute-start | bytes 393224 | tf_op jit(solution)/shard_map/ppermute | solution.py:269
  18.4 0.9 %copy-start = (bf16[1,512,128]{2,1,0:T(8,128)(2,1)S(1)}, bf16[1,512,128]{2,1,0:T(8,128)(2,1)}, u32[]{:S(2)}) copy-start(bf16[1,512,128]{2,1,0:T(8,128)(2,1)} %param.5) | copy-start | bytes 393220
  21.4 9.8 %all-to-all-start.1 = ((bf16[16,32,128]{2,1,0:T(8,128)(2,1)}), bf16[16,32,128]{2,1,0:T(8,128)(2,1)S(1)}, u32[]{:S(2)}, u32[]{:S(2)}) async-start(bf16[16,32,128]{2,1,0:T(8,128)(2,1)} %bitcast.8), calls=%async_computation.1 | async-start | bytes 262144 | tf_op jit(solution)/shard_map/all_to_all | solution.py:322
  28.1 1.4 %collective-permute-start.4 = (bf16[528,128]{1,0:T(8,128)(2,1)S(1)}, bf16[528,128]{1,0:T(8,128)(2,1)S(1)}, u32[]{:S(2)}, u32[]{:S(2)}) collective-permute-start(bf16[528,128]{1,0:T(8,128)(2,1)S(1)} %get-tuple-element.16), channel_id=1, source_target_pairs={{0,2},{2,0},{4,6},{6,4},{8,10},{10,8},{12,14},{14,12},{16,18},{18,... | collective-permute-start | bytes 405512 | tf_op jit(solution)/shard_map/ppermute | solution.py:340

commit v6 on v5

--- a/solution.py
+++ b/solution.py
@@ -18,6 +18,17 @@
 TAIL = 16
 SHIFT = 1
 VMEM_BYTES = 24 * 2**20
+
+
+def chip_at(place, chips):
+    half = chips // 2
+    step = 1 if half % 2 else 2
+    down = place - half
+    if isinstance(place, int):
+        return place + half if down < 0 else step * (half // step - 1 - down // step) + down % step
+    down = jnp.maximum(down, 0)
+    lower = step * (half // step - 1 - lax.div(down, step)) + lax.rem(down, step)
+    return jnp.where(place < half, place + half, lower)
 
 
 def over_tokens(left, right):
@@ -142,7 +153,7 @@
         one, two = (
             Page(
                 query_len, page_len, query_rows, a, b, bias_ref[2 * k], bias_ref[2 * k + 1],
-                sign_ref[k : k + 1, pl.ds(offset, block_rows)],
+                sign_ref[0, k : k + 1, pl.ds(offset, block_rows)],
             )
             for k, (a, b) in enumerate(((near, far), (near2, far2)))
         )
@@ -150,7 +161,8 @@
         dests = block_rows // dest_rows
         shaped = terms.T.astype(jnp.bfloat16).reshape(dests, dest_rows, width)
         for d in range(dests):
-            place = lax.rem(index * dests + d + held.shape[0] - SHIFT, held.shape[0])
+            chips = held.shape[0]
+            place = (chip_at(index * dests + d, chips) + chips - chips // 2 - SHIFT) % chips
             for k in range(copies):
                 held[place, k] = shaped[d]
         for k, page in enumerate((one, two)):
@@ -190,7 +202,7 @@
         one, two = (
             Page(
                 query_len, page_len, query_rows, a[...], b[...], bias_ref[2 * k], bias_ref[2 * k + 1],
-                sign_ref[k : k + 1, pl.ds(offset, block_rows)],
+                sign_ref[1, k : k + 1, pl.ds(offset, block_rows)],
             )
             for k, (a, b) in enumerate(((near_ref, far_ref), (near2_ref, far2_ref)))
         )
@@ -207,13 +219,32 @@
     sent_ref[pl.ds(tokens, TAIL), :] = loss_parts(jnp.max(losses[1:2]))
 
 
-def bias_body(limits_ref, bias_ref):
-    shape = bias_ref.shape[1:]
-    row = lax.broadcasted_iota(jnp.int32, shape, 0)
-    lane = lax.broadcasted_iota(jnp.int32, shape, 1)
-    for k in range(bias_ref.shape[0]):
-        padding = (row >= limits_ref[k]) & (lane == 0)
-        bias_ref[k] = jnp.where(padding, MASKED, 0.0).astype(jnp.bfloat16)
+def bias_body(query_count, query_len, facts_ref, facts2_ref, bias_ref, sign_ref):
+    tokens = bias_ref.shape[1]
+    shares, _, row_count = sign_ref.shape
+    share = lax.axis_index("tok")
+    side = lax.rem(lax.axis_index("pages"), 2)
+    picked = query_count // shares
+    chips = row_count // (picked * query_len)
+    row = lax.broadcasted_iota(jnp.int32, bias_ref.shape[1:], 0)
+    lane = lax.broadcasted_iota(jnp.int32, bias_ref.shape[1:], 1)
+    group = lax.broadcasted_iota(jnp.int32, (1, LANES), 1) // query_len
+    for page, ref in enumerate((facts_ref, facts2_ref)):
+        usable = shares * tokens - ref[ref.shape[0] - 1]
+        for half in range(shares):
+            first = lax.rem(share + half, shares) * tokens
+            padding = (row >= usable - first) & (lane == 0)
+            bias_ref[shares * page + half] = jnp.where(padding, MASKED, 0.0).astype(jnp.bfloat16)
+        for slot in range(shares):
+            start = lax.rem(share + slot, shares) * picked
+            for piece in range(row_count // LANES):
+                signs = jnp.zeros((1, LANES), jnp.float32)
+                for k in range(LANES // query_len):
+                    place = piece * (LANES // query_len) + k
+                    chip = chip_at(place // picked, chips)
+                    label = ref[(2 * chip + side) * query_count + start + place % picked]
+                    signs = jnp.where(group == k, 2.0 * label.astype(jnp.float32) - 1.0, signs)
+                sign_ref[slot, page : page + 1, pl.ds(piece * LANES, LANES)] = signs
 
 
 def last_body(near_ref, loss_ref, got_ref, grad_ref, total_ref):
@@ -230,17 +261,15 @@
     if shares != 2 or query_count % shares or owners % 2:
         raise ValueError("unsupported split")
     share = lax.axis_index("tok")
-    side = lax.axis_index("pages") % 2
     page_len = tokens * shares
     picked = query_count // shares
     dest_rows = picked * query_len
     chips = owners // 2
     swap = [(0, 1), (1, 0)]
     partner = [(i, i ^ 1) for i in range(owners)]
-    turn = chips // 2
-    order = [(j + turn) % chips for j in range(chips)]
+    order = [chip_at(j, chips) for j in range(chips)]
     same_side = [[2 * j + c for j in order] for c in range(2)]
-    later = order[SHIFT:] + order[:SHIFT]
+    later = [(j + chips // 2 + SHIFT) % chips for j in range(chips)]
     same_side_all = [
         [(2 * j + c) * shares + k for j in later for k in range(shares)] for c in range(2)
     ]
@@ -269,31 +298,27 @@
     far2 = lax.ppermute(far, "pages", partner)
     facts = jnp.concatenate([labels[:, 0], pad_counts])
     facts2 = lax.ppermute(facts, "pages", partner)
-    both = jnp.stack([facts, facts2])
-    usable = page_len - both[:, -1:]
-    limits = jnp.concatenate([usable - share * tokens, usable - (1 - share) * tokens], axis=1).reshape(4)
-    label = jnp.roll(both[:, :-1].reshape(2, chips, 2, shares, picked), -turn, axis=1)
-    label = 2.0 * lax.dynamic_index_in_dim(label, side, 2, False).astype(jnp.float32) - 1.0
 
     def of_share(index):
-        rows = lax.dynamic_index_in_dim(gathered, index, 1, False).reshape(row_count, width)
-        sign = lax.dynamic_index_in_dim(label, index, 2, False).reshape(2, chips * picked)
-        return rows, jnp.repeat(sign, query_len, axis=1)
+        return lax.dynamic_index_in_dim(gathered, index, 1, False).reshape(row_count, width)
 
     row_count = chips * dest_rows
-    rows, sign = of_share(share)
-    rows_b, sign_b = of_share(1 - share)
+    rows = of_share(share)
+    rows_b = of_share(1 - share)
     half = jax.ShapeDtypeStruct((tokens, width), jnp.float32)
     lane_row = jax.ShapeDtypeStruct((8, LANES), jnp.float32)
-    bias = pl.pallas_call(
-        bias_body,
-        out_shape=jax.ShapeDtypeStruct((4, tokens, LANES), jnp.bfloat16),
-        in_specs=[smem],
-        out_specs=vmem,
+    bias, signs = pl.pallas_call(
+        functools.partial(bias_body, query_count, query_len),
+        out_shape=(
+            jax.ShapeDtypeStruct((2 * shares, tokens, LANES), jnp.bfloat16),
+            jax.ShapeDtypeStruct((shares, 2, row_count), jnp.float32),
+        ),
+        in_specs=[smem, smem],
+        out_specs=(vmem, vmem),
         cost_estimate=pl.CostEstimate(flops=0, transcendentals=0, bytes_accessed=8 * tokens * width),
         compiler_params=params,
         name="page_bias",
-    )(limits)
+    )(facts, facts2)
     block_rows = math.gcd(row_count, ROW_BLOCK)
     blocks, sums, loss = pl.pallas_call(
         functools.partial(step_body, query_len, page_len),
@@ -317,7 +342,7 @@
         ),
         compiler_params=params,
         name="page_step",
-    )(bias, rows, near, far, near2, far2, sign)
+    )(bias, rows, near, far, near2, far2, signs)
 
     partials = lax.all_to_all(
         blocks.reshape(chips * shares, dest_rows, width),
@@ -336,7 +361,7 @@
         ),
         compiler_params=params,
         name="page_rest",
-    )(bias, rows_b, near, far, near2, far2, sign_b, sums, loss)
+    )(bias, rows_b, near, far, near2, far2, signs, sums, loss)
     got = lax.ppermute(sent, "pages", partner)
     page_grad, page_loss = pl.pallas_call(
         last_body,

time: 32.3 us -> 29 us (0.90)
  local copies, waits for them, and re-layouts: 2.96 us -> 0.8 us
  waiting for transfers between devices: 5.62 us -> 4.2 us
  starting transfers between devices: 15.2 us -> 15.8 us
    all_to_all x1, waiting for transfers between devices: 3.34 us -> 0.96 us  [device_step(): lax.all_to_all(asked.reshape(chips, query_count * query_len, width), 'pag...]
    unnamed x6, local copies, waits for them, and re-layouts: 2.24 us -> 0.79 us
    ppermute x1, waiting for transfers between devices: 0.01 us -> 0.82 us  [device_step(): facts2 = lax.ppermute(facts, 'pages', partner)]
    ppermute x1, starting transfers between devices: 0.07 us -> 0.57 us  [device_step(): far2 = lax.ppermute(far, 'pages', partner)]
    reshape x4 -> x0, local copies, waits for them, and re-layouts: 0.34 us -> none  [the longest x2 0.16 us: of_share(): return (rows, jnp.repeat(sign, query_len, axis=1))]
  transfers between devices with their start and end apart: 7 -> 7, of which waited for: 3 -> 4; matrix products, arithmetic and copies ran while one was open for 3% -> 0% of each run, Pallas kernels for 11% -> 13%
where the time goes in v6:
time: 29 us; the launch traced here: 28.6 us
  starting transfers between devices  15.8 us (54%)
  Pallas kernels  5.64 us (19%)
  waiting for transfers between devices  4.2 us (14%)
  between operations  1.38 us (5%)
  local copies, waits for them, and re-layouts  0.8 us (3%)
  other arithmetic  0.72 us (2%)
    all_to_all x1, starting transfers between devices, device_step(): lax.all_to_all(asked.reshape(chips, query_count * query_len, width), 'pag...  6.51 us
    all_to_all x1, starting transfers between devices, device_step(): lax.all_to_all(blocks.reshape(chips * shares, dest_rows, width), ('pages'...  5.13 us
    ppermute x1, starting transfers between devices, device_step(): far = lax.ppermute(near, 'tok', swap)  3.06 us
    pallas_call x1, Pallas kernels, device_step(): pl.pallas_call(functools.partial(step_body, query_len, page_len), out_sha...  2.06 us
    pallas_call x1, Pallas kernels, device_step(): pl.pallas_call(functools.partial(rest_body, query_len, page_len), out_sha...  1.47 us
    ppermute x1, waiting for transfers between devices, device_step(): got = lax.ppermute(sent, 'pages', partner)  1.34 us
    all_to_all x1, waiting for transfers between devices, device_step(): lax.all_to_all(blocks.reshape(chips * shares, dest_rows, width), ('pages'...  1.07 us
    all_to_all x1, waiting for transfers between devices, device_step(): lax.all_to_all(asked.reshape(chips, query_count * query_len, width), 'pag...  0.96 us
  transfers between devices with their start and end apart: 7, of which 4 were waited for; matrix products, arithmetic and copies ran while one was open for 0% of the time, Pallas kernels for 13%

profile of v6, /device:TPU:0, one launch (start us, length us, event | category | flops | bytes accessed | tf_op | source)
XLA Modules:
  0.0 28.6 jit_solution(2996347135844165587)
XLA Ops:
  0.6 3.1 %collective-permute-start.1 = (bf16[512,128]{1,0:T(8,128)(2,1)}, bf16[512,128]{1,0:T(8,128)(2,1)S(1)}, u32[]{:S(2)}, u32[]{:S(2)}) collective-permute-start(bf16[512,128]{1,0:T(8,128)(2,1)} %bitcast.10), channel_id=1, source_target_pairs={{0,1},{1,0},{2,3},{3,2},{4,5},{5,4},{6,7},{7,6},{8,9},{9,8},{10,11... | collective-permute-start | bytes 393224 | tf_op jit(solution)/shard_map/ppermute | solution.py:296
  3.7 0.0 copy-start.1
  3.7 0.7 %copy-done.1 = bf16[2,32,128]{2,1,0:T(8,128)(2,1)S(1)} copy-done((bf16[2,32,128]{2,1,0:T(8,128)(2,1)S(1)}, bf16[2,32,128]{2,1,0:T(8,128)(2,1)}, u32[]{:S(2)}) %copy-start.1) | copy-done | bytes 16408
  4.4 0.7 %ask_copies.1 = bf16[8,2,32,128]{3,2,1,0:T(8,128)(2,1)} custom-call(bf16[2,32,128]{2,1,0:T(8,128)(2,1)S(1)} %copy-done.1), custom_call_target="tpu_custom_call" | custom-call | tf_op jit(solution)/shard_map/ask_copies/pallas_call | solution.py:281
  5.1 0.0 copy-start
  5.1 6.5 %all-to-all-start = ((bf16[8,64,128]{2,1,0:T(8,128)(2,1)}), bf16[8,64,128]{2,1,0:T(8,128)(2,1)S(1)}, u32[]{:S(2)}, u32[]{:S(2)}) async-start(bf16[8,64,128]{2,1,0:T(8,128)(2,1)} %bitcast.1), calls=%async_computation | async-start | bytes 262144 | tf_op jit(solution)/shard_map/all_to_all | solution.py:290
  11.7 0.0 copy-done
  11.7 0.0 collective-permute-start.2
  12.3 0.0 copy-start.2
  12.3 0.0 collective-permute-done.1.far_ref
  12.3 0.6 %collective-permute-start.3 = (bf16[512,128]{1,0:T(8,128)(2,1)S(1)}, bf16[512,128]{1,0:T(8,128)(2,1)S(1)}, u32[]{:S(2)}, u32[]{:S(2)}) collective-permute-start(bf16[512,128]{1,0:T(8,128)(2,1)S(1)} %collective-permute-done.1.far_ref), channel_id=1, source_target_pairs={{0,2},{2,0},{4,6},{6,4},{8,10},{10,8},{12,14},{14,12},{16,18},{18,... | collective-permute-start | bytes 393224 | tf_op jit(solution)/shard_map/ppermute | solution.py:298
  12.9 0.1 copy-done.2
  13.0 0.1 pad_add_fusion.facts_ref
  13.0 0.5 %collective-permute-start = (s32[33]{0:T(128)S(1)}, s32[33]{0:T(128)S(1)}, u32[]{:S(2)}, u32[]{:S(2)}) collective-permute-start(s32[33]{0:T(128)S(1)} %pad_add_fusion.facts_ref), channel_id=1, source_target_pairs={{0,2},{2,0},{4,6},{6,4},{8,10},{10,8},{12,14},{14,12},{16,18},{18,... | collective-permute-start | bytes 404 | tf_op jit(solution)/shard_map/ppermute | solution.py:300
  13.5 0.8 %collective-permute-done.facts2_ref = s32[33]{0:T(128)S(1)} collective-permute-done((s32[33]{0:T(128)S(1)}, s32[33]{0:T(128)S(1)}, u32[]{:S(2)}, u32[]{:S(2)}) %collective-permute-start) | collective-permute-done | bytes 164 | tf_op jit(solution)/shard_map/ppermute | solution.py:300
  14.4 0.7 %page_bias.1 = (bf16[4,512,128]{2,1,0:T(8,128)(2,1)S(1)}, f32[2,2,256]{2,1,0:T(2,128)S(1)}) custom-call(s32[33]{0:T(128)S(1)} %pad_add_fusion.facts_ref, s32[33]{0:T(128)S(1)} %collective-permute-done.facts2_ref), custom_call_target="tpu_custom_call" | custom-call | bytes 524288 | tf_op jit(solution)/shard_map/page_bias/pallas_call | solution.py:310
  15.0 1.0 %all-to-all-done = bf16[8,64,128]{2,1,0:T(8,128)(2,1)S(1)} async-done(((bf16[8,64,128]{2,1,0:T(8,128)(2,1)}), bf16[8,64,128]{2,1,0:T(8,128)(2,1)S(1)}, u32[]{:S(2)}, u32[]{:S(2)}) %all-to-all-start) | async-done | bytes 131104 | tf_op jit(solution)/shard_map/all_to_all | solution.py:290
  16.0 0.0 collective-permute-done.2.near2_ref
  16.0 0.0 collective-permute-done.3.far2_ref
  16.0 2.1 %page_step.1 = (bf16[8,2,32,128]{3,2,1,0:T(8,128)(2,1)}, f32[2,512,128]{2,1,0:T(8,128)S(1)}, f32[8,128]{1,0:T(8,128)S(1)}) custom-call(bf16[4,512,128]{2,1,0:T(8,128)(2,1)S(1)} %get-tuple-element.13.bias_ref, bf16[256,128]{1,0:T(8,128)(2,1)S(1)} %bitcast.14, bf16[512,128]{1,0:T(8,128)(2,1)S(1)} %bitcast.12, ...), custom_call_target="tpu_custom_call" | custom-call | flops 335544320 | bytes 1507328 | tf_op jit(solution)/shard_map/page_step/pallas_call | solution.py:323
  18.1 5.1 %all-to-all-start.1 = ((bf16[16,32,128]{2,1,0:T(8,128)(2,1)}), bf16[16,32,128]{2,1,0:T(8,128)(2,1)S(1)}, u32[]{:S(2)}, u32[]{:S(2)}) async-start(bf16[16,32,128]{2,1,0:T(8,128)(2,1)} %bitcast.5), calls=%async_computation.1 | async-start | bytes 262144 | tf_op jit(solution)/shard_map/all_to_all | solution.py:347
  23.2 1.5 %page_rest.1 = (f32[512,128]{1,0:T(8,128)S(1)}, bf16[528,128]{1,0:T(8,128)(2,1)S(1)}, f32[8,128]{1,0:T(8,128)S(1)}) custom-call(bf16[4,512,128]{2,1,0:T(8,128)(2,1)S(1)} %get-tuple-element.13.bias_ref, bf16[256,128]{1,0:T(8,128)(2,1)S(1)} %bitcast.9, bf16[512,128]{1,0:T(8,128)(2,1)S(1)} %bitcast.13, bf16[512,128]{1,0:T(8,128)(2,1)S(1)} %collective-permute-done.1.far_ref, ...), custom_call_target="tpu_custom_call" | custom-call | flops 201326592 | bytes 1376256 | tf_op jit(solution)/shard_map/page_rest/pallas_call | solution.py:351
  24.7 0.1 collective-permute-start.4
  24.8 1.3 %collective-permute-done.4.got_ref = bf16[528,128]{1,0:T(8,128)(2,1)S(1)} collective-permute-done((bf16[528,128]{1,0:T(8,128)(2,1)S(1)}, bf16[528,128]{1,0:T(8,128)(2,1)S(1)}, u32[]{:S(2)}, u32[]{:S(2)}) %collective-permute-start.4) | collective-permute-done | bytes 135200 | tf_op jit(solution)/shard_map/ppermute | solution.py:365
  26.1 0.7 %page_out.1 = (f32[1,512,128]{2,1,0:T(8,128)}, f32[1]{0:T(128)}) custom-call(f32[512,128]{1,0:T(8,128)S(1)} %get-tuple-element.18.near_ref, f32[8,128]{1,0:T(8,128)S(1)} %get-tuple-element.19.loss_ref, bf16[528,128]{1,0:T(8,128)(2,1)S(1)} %collective-permute-done.4.got_ref), custom_call_target="tpu_custom_call" | custom-call | flops 131072 | bytes 786432 | tf_op jit(solution)/shard_map/page_out/pallas_call | solution.py:366
  26.9 1.1 %all-to-all-done.1 = bf16[16,32,128]{2,1,0:T(8,128)(2,1)S(1)} async-done(((bf16[16,32,128]{2,1,0:T(8,128)(2,1)}), bf16[16,32,128]{2,1,0:T(8,128)(2,1)S(1)}, u32[]{:S(2)}, u32[]{:S(2)}) %all-to-all-start.1) | async-done | bytes 131104 | tf_op jit(solution)/shard_map/all_to_all | solution.py:347
  28.0 0.6 %broadcast_multiply_fusion = f32[2,32,128]{2,1,0:T(8,128)} fusion(f32[2,32,128]{2,1,0:T(8,128)S(1)} %convert_reduce_fusion), kind=kLoop, calls=%fused_computation.1 | loop fusion | flops 8192 | bytes 65536 | tf_op jit(solution)/shard_map/mul | solution.py:378
  (2 shorter events, 0.0 us)
Async XLA Ops:
  0.6 11.7 %collective-permute-start.1 = (bf16[512,128]{1,0:T(8,128)(2,1)}, bf16[512,128]{1,0:T(8,128)(2,1)S(1)}, u32[]{:S(2)}, u32[]{:S(2)}) collective-permute-start(bf16[512,128]{1,0:T(8,128)(2,1)} %bitcast.10), channel_id=1, source_target_pairs={{0,1},{1,0},{2,3},{3,2},{4,5},{5,4},{6,7},{7,6},{8,9},{9,8},{10,11... | collective-permute-start | bytes 393224 | tf_op jit(solution)/shard_map/ppermute | solution.py:296
  3.7 0.7 %copy-start.1 = (bf16[2,32,128]{2,1,0:T(8,128)(2,1)S(1)}, bf16[2,32,128]{2,1,0:T(8,128)(2,1)}, u32[]{:S(2)}) copy-start(bf16[2,32,128]{2,1,0:T(8,128)(2,1)} %queries_ref.1) | copy-start | bytes 49156
  5.1 6.5 %copy-start = (bf16[1,512,128]{2,1,0:T(8,128)(2,1)S(1)}, bf16[1,512,128]{2,1,0:T(8,128)(2,1)}, u32[]{:S(2)}) copy-start(bf16[1,512,128]{2,1,0:T(8,128)(2,1)} %param.5) | copy-start | bytes 393220
  5.1 10.9 %all-to-all-start = ((bf16[8,64,128]{2,1,0:T(8,128)(2,1)}), bf16[8,64,128]{2,1,0:T(8,128)(2,1)S(1)}, u32[]{:S(2)}, u32[]{:S(2)}) async-start(bf16[8,64,128]{2,1,0:T(8,128)(2,1)} %bitcast.1), calls=%async_computation | async-start | bytes 262144 | tf_op jit(solution)/shard_map/all_to_all | solution.py:290
  11.7 4.4 %collective-permute-start.2 = (bf16[512,128]{1,0:T(8,128)(2,1)S(1)}, bf16[512,128]{1,0:T(8,128)(2,1)S(1)}, u32[]{:S(2)}, u32[]{:S(2)}) collective-permute-start(bf16[512,128]{1,0:T(8,128)(2,1)S(1)} %bitcast.11), channel_id=1, source_target_pairs={{0,2},{2,0},{4,6},{6,4},{8,10},{10,8},{12,14},{14,12},{16,18},{18,... | collective-permute-start | bytes 393224 | tf_op jit(solution)/shard_map/ppermute | solution.py:297
  12.3 0.7 %copy-start.2 = (s32[32,1]{0,1:T(1,128)S(1)}, s32[32,1]{0,1:T(1,128)}, u32[]{:S(2)}) copy-start(s32[32,1]{0,1:T(1,128)} %param.7) | copy-start | bytes 388
  12.3 3.7 %collective-permute-start.3 = (bf16[512,128]{1,0:T(8,128)(2,1)S(1)}, bf16[512,128]{1,0:T(8,128)(2,1)S(1)}, u32[]{:S(2)}, u32[]{:S(2)}) collective-permute-start(bf16[512,128]{1,0:T(8,128)(2,1)S(1)} %collective-permute-done.1.far_ref), channel_id=1, source_target_pairs={{0,2},{2,0},{4,6},{6,4},{8,10},{10,8},{12,14},{14,12},{16,18},{18,... | collective-permute-start | bytes 393224 | tf_op jit(solution)/shard_map/ppermute | solution.py:298
  13.0 1.3 %collective-permute-start = (s32[33]{0:T(128)S(1)}, s32[33]{0:T(128)S(1)}, u32[]{:S(2)}, u32[]{:S(2)}) collective-permute-start(s32[33]{0:T(128)S(1)} %pad_add_fusion.facts_ref), channel_id=1, source_target_pairs={{0,2},{2,0},{4,6},{6,4},{8,10},{10,8},{12,14},{14,12},{16,18},{18,... | collective-permute-start | bytes 404 | tf_op jit(solution)/shard_map/ppermute | solution.py:300
  18.1 9.8 %all-to-all-start.1 = ((bf16[16,32,128]{2,1,0:T(8,128)(2,1)}), bf16[16,32,128]{2,1,0:T(8,128)(2,1)S(1)}, u32[]{:S(2)}, u32[]{:S(2)}) async-start(bf16[16,32,128]{2,1,0:T(8,128)(2,1)} %bitcast.5), calls=%async_computation.1 | async-start | bytes 262144 | tf_op jit(solution)/shard_map/all_to_all | solution.py:347
  24.7 1.4 %collective-permute-start.4 = (bf16[528,128]{1,0:T(8,128)(2,1)S(1)}, bf16[528,128]{1,0:T(8,128)(2,1)S(1)}, u32[]{:S(2)}, u32[]{:S(2)}) collective-permute-start(bf16[528,128]{1,0:T(8,128)(2,1)S(1)} %get-tuple-element.20), channel_id=1, source_target_pairs={{0,2},{2,0},{4,6},{6,4},{8,10},{10,8},{12,14},{14,12},{16,18},{18,... | collective-permute-start | bytes 405512 | tf_op jit(solution)/shard_map/ppermute | solution.py:365

commit v7 on v6

--- a/solution.py
+++ b/solution.py
@@ -277,6 +277,7 @@
     smem = pl.BlockSpec(memory_space=pltpu.SMEM)
     anywhere = pl.BlockSpec(memory_space=pl.ANY)
     params = pltpu.CompilerParams(vmem_limit_bytes=VMEM_BYTES)
+    packed = pltpu.CompilerParams(vmem_limit_bytes=VMEM_BYTES)
 
     asked = pl.pallas_call(
         ask_body,
@@ -340,7 +341,7 @@
             transcendentals=2 * row_count * page_len,
             bytes_accessed=6 * row_count * width + 20 * tokens * width,
         ),
-        compiler_params=params,
+        compiler_params=packed,
         name="page_step",
     )(bias, rows, near, far, near2, far2, signs)
 
@@ -359,7 +360,7 @@
             transcendentals=2 * row_count * page_len,
             bytes_accessed=2 * row_count * width + 20 * tokens * width,
         ),
-        compiler_params=params,
+        compiler_params=packed,
         name="page_rest",
     )(bias, rows_b, near, far, near2, far2, signs, sums, loss)
     got = lax.ppermute(sent, "pages", partner)

time: 29 us -> 29 us (level)
  no operation moved by 1% of the time
where the time goes in v7:
time: 29 us; the launch traced here: 28.6 us
  starting transfers between devices  15.8 us (54%)
  Pallas kernels  5.64 us (19%)
  waiting for transfers between devices  4.2 us (14%)
  between operations  1.38 us (5%)
  local copies, waits for them, and re-layouts  0.8 us (3%)
  other arithmetic  0.72 us (2%)
    all_to_all x1, starting transfers between devices, device_step(): lax.all_to_all(asked.reshape(chips, query_count * query_len, width), 'pag...  6.51 us
    all_to_all x1, starting transfers between devices, device_step(): lax.all_to_all(blocks.reshape(chips * shares, dest_rows, width), ('pages'...  5.13 us
    ppermute x1, starting transfers between devices, device_step(): far = lax.ppermute(near, 'tok', swap)  3.06 us
    pallas_call x1, Pallas kernels, device_step(): pl.pallas_call(functools.partial(step_body, query_len, page_len), out_sha...  2.06 us
    pallas_call x1, Pallas kernels, device_step(): pl.pallas_call(functools.partial(rest_body, query_len, page_len), out_sha...  1.47 us
    ppermute x1, waiting for transfers between devices, device_step(): got = lax.ppermute(sent, 'pages', partner)  1.34 us
    all_to_all x1, waiting for transfers between devices, device_step(): lax.all_to_all(blocks.reshape(chips * shares, dest_rows, width), ('pages'...  1.07 us
    all_to_all x1, waiting for transfers between devices, device_step(): lax.all_to_all(asked.reshape(chips, query_count * query_len, width), 'pag...  0.96 us
  transfers between devices with their start and end apart: 7, of which 4 were waited for; matrix products, arithmetic and copies ran while one was open for 0% of the time, Pallas kernels for 13%

profile of v7, /device:TPU:0, one launch (start us, length us, event | category | flops | bytes accessed | tf_op | source)
XLA Modules:
  0.0 28.6 jit_solution(2996347135844165587)
XLA Ops:
  0.6 3.1 %collective-permute-start.1 = (bf16[512,128]{1,0:T(8,128)(2,1)}, bf16[512,128]{1,0:T(8,128)(2,1)S(1)}, u32[]{:S(2)}, u32[]{:S(2)}) collective-permute-start(bf16[512,128]{1,0:T(8,128)(2,1)} %bitcast.10), channel_id=1, source_target_pairs={{0,1},{1,0},{2,3},{3,2},{4,5},{5,4},{6,7},{7,6},{8,9},{9,8},{10,11... | collective-permute-start | bytes 393224 | tf_op jit(solution)/shard_map/ppermute | solution.py:297
  3.7 0.0 copy-start.1
  3.7 0.7 %copy-done.1 = bf16[2,32,128]{2,1,0:T(8,128)(2,1)S(1)} copy-done((bf16[2,32,128]{2,1,0:T(8,128)(2,1)S(1)}, bf16[2,32,128]{2,1,0:T(8,128)(2,1)}, u32[]{:S(2)}) %copy-start.1) | copy-done | bytes 16408
  4.4 0.7 %ask_copies.1 = bf16[8,2,32,128]{3,2,1,0:T(8,128)(2,1)} custom-call(bf16[2,32,128]{2,1,0:T(8,128)(2,1)S(1)} %copy-done.1), custom_call_target="tpu_custom_call" | custom-call | tf_op jit(solution)/shard_map/ask_copies/pallas_call | solution.py:282
  5.1 0.0 copy-start
  5.1 6.5 %all-to-all-start = ((bf16[8,64,128]{2,1,0:T(8,128)(2,1)}), bf16[8,64,128]{2,1,0:T(8,128)(2,1)S(1)}, u32[]{:S(2)}, u32[]{:S(2)}) async-start(bf16[8,64,128]{2,1,0:T(8,128)(2,1)} %bitcast.1), calls=%async_computation | async-start | bytes 262144 | tf_op jit(solution)/shard_map/all_to_all | solution.py:291
  11.7 0.0 copy-done
  11.7 0.0 collective-permute-start.2
  12.3 0.0 copy-start.2
  12.3 0.0 collective-permute-done.1.far_ref
  12.3 0.6 %collective-permute-start.3 = (bf16[512,128]{1,0:T(8,128)(2,1)S(1)}, bf16[512,128]{1,0:T(8,128)(2,1)S(1)}, u32[]{:S(2)}, u32[]{:S(2)}) collective-permute-start(bf16[512,128]{1,0:T(8,128)(2,1)S(1)} %collective-permute-done.1.far_ref), channel_id=1, source_target_pairs={{0,2},{2,0},{4,6},{6,4},{8,10},{10,8},{12,14},{14,12},{16,18},{18,... | collective-permute-start | bytes 393224 | tf_op jit(solution)/shard_map/ppermute | solution.py:299
  12.9 0.1 copy-done.2
  13.0 0.1 pad_add_fusion.facts_ref
  13.0 0.5 %collective-permute-start = (s32[33]{0:T(128)S(1)}, s32[33]{0:T(128)S(1)}, u32[]{:S(2)}, u32[]{:S(2)}) collective-permute-start(s32[33]{0:T(128)S(1)} %pad_add_fusion.facts_ref), channel_id=1, source_target_pairs={{0,2},{2,0},{4,6},{6,4},{8,10},{10,8},{12,14},{14,12},{16,18},{18,... | collective-permute-start | bytes 404 | tf_op jit(solution)/shard_map/ppermute | solution.py:301
  13.5 0.8 %collective-permute-done.facts2_ref = s32[33]{0:T(128)S(1)} collective-permute-done((s32[33]{0:T(128)S(1)}, s32[33]{0:T(128)S(1)}, u32[]{:S(2)}, u32[]{:S(2)}) %collective-permute-start) | collective-permute-done | bytes 164 | tf_op jit(solution)/shard_map/ppermute | solution.py:301
  14.4 0.7 %page_bias.1 = (bf16[4,512,128]{2,1,0:T(8,128)(2,1)S(1)}, f32[2,2,256]{2,1,0:T(2,128)S(1)}) custom-call(s32[33]{0:T(128)S(1)} %pad_add_fusion.facts_ref, s32[33]{0:T(128)S(1)} %collective-permute-done.facts2_ref), custom_call_target="tpu_custom_call" | custom-call | bytes 524288 | tf_op jit(solution)/shard_map/page_bias/pallas_call | solution.py:311
  15.0 1.0 %all-to-all-done = bf16[8,64,128]{2,1,0:T(8,128)(2,1)S(1)} async-done(((bf16[8,64,128]{2,1,0:T(8,128)(2,1)}), bf16[8,64,128]{2,1,0:T(8,128)(2,1)S(1)}, u32[]{:S(2)}, u32[]{:S(2)}) %all-to-all-start) | async-done | bytes 131104 | tf_op jit(solution)/shard_map/all_to_all | solution.py:291
  16.0 0.0 collective-permute-done.2.near2_ref
  16.0 0.0 collective-permute-done.3.far2_ref
  16.0 2.1 %page_step.1 = (bf16[8,2,32,128]{3,2,1,0:T(8,128)(2,1)}, f32[2,512,128]{2,1,0:T(8,128)S(1)}, f32[8,128]{1,0:T(8,128)S(1)}) custom-call(bf16[4,512,128]{2,1,0:T(8,128)(2,1)S(1)} %get-tuple-element.13.bias_ref, bf16[256,128]{1,0:T(8,128)(2,1)S(1)} %bitcast.14, bf16[512,128]{1,0:T(8,128)(2,1)S(1)} %bitcast.12, ...), custom_call_target="tpu_custom_call" | custom-call | flops 335544320 | bytes 1507328 | tf_op jit(solution)/shard_map/page_step/pallas_call | solution.py:324
  18.1 5.1 %all-to-all-start.1 = ((bf16[16,32,128]{2,1,0:T(8,128)(2,1)}), bf16[16,32,128]{2,1,0:T(8,128)(2,1)S(1)}, u32[]{:S(2)}, u32[]{:S(2)}) async-start(bf16[16,32,128]{2,1,0:T(8,128)(2,1)} %bitcast.5), calls=%async_computation.1 | async-start | bytes 262144 | tf_op jit(solution)/shard_map/all_to_all | solution.py:348
  23.2 1.5 %page_rest.1 = (f32[512,128]{1,0:T(8,128)S(1)}, bf16[528,128]{1,0:T(8,128)(2,1)S(1)}, f32[8,128]{1,0:T(8,128)S(1)}) custom-call(bf16[4,512,128]{2,1,0:T(8,128)(2,1)S(1)} %get-tuple-element.13.bias_ref, bf16[256,128]{1,0:T(8,128)(2,1)S(1)} %bitcast.9, bf16[512,128]{1,0:T(8,128)(2,1)S(1)} %bitcast.13, bf16[512,128]{1,0:T(8,128)(2,1)S(1)} %collective-permute-done.1.far_ref, ...), custom_call_target="tpu_custom_call" | custom-call | flops 201326592 | bytes 1376256 | tf_op jit(solution)/shard_map/page_rest/pallas_call | solution.py:352
  24.7 0.1 collective-permute-start.4
  24.8 1.3 %collective-permute-done.4.got_ref = bf16[528,128]{1,0:T(8,128)(2,1)S(1)} collective-permute-done((bf16[528,128]{1,0:T(8,128)(2,1)S(1)}, bf16[528,128]{1,0:T(8,128)(2,1)S(1)}, u32[]{:S(2)}, u32[]{:S(2)}) %collective-permute-start.4) | collective-permute-done | bytes 135200 | tf_op jit(solution)/shard_map/ppermute | solution.py:366
  26.1 0.7 %page_out.1 = (f32[1,512,128]{2,1,0:T(8,128)}, f32[1]{0:T(128)}) custom-call(f32[512,128]{1,0:T(8,128)S(1)} %get-tuple-element.18.near_ref, f32[8,128]{1,0:T(8,128)S(1)} %get-tuple-element.19.loss_ref, bf16[528,128]{1,0:T(8,128)(2,1)S(1)} %collective-permute-done.4.got_ref), custom_call_target="tpu_custom_call" | custom-call | flops 131072 | bytes 786432 | tf_op jit(solution)/shard_map/page_out/pallas_call | solution.py:367
  26.9 1.1 %all-to-all-done.1 = bf16[16,32,128]{2,1,0:T(8,128)(2,1)S(1)} async-done(((bf16[16,32,128]{2,1,0:T(8,128)(2,1)}), bf16[16,32,128]{2,1,0:T(8,128)(2,1)S(1)}, u32[]{:S(2)}, u32[]{:S(2)}) %all-to-all-start.1) | async-done | bytes 131104 | tf_op jit(solution)/shard_map/all_to_all | solution.py:348
  28.0 0.6 %broadcast_multiply_fusion = f32[2,32,128]{2,1,0:T(8,128)} fusion(f32[2,32,128]{2,1,0:T(8,128)S(1)} %convert_reduce_fusion), kind=kLoop, calls=%fused_computation.1 | loop fusion | flops 8192 | bytes 65536 | tf_op jit(solution)/shard_map/mul | solution.py:379
  (2 shorter events, 0.0 us)
Async XLA Ops:
  0.6 11.7 %collective-permute-start.1 = (bf16[512,128]{1,0:T(8,128)(2,1)}, bf16[512,128]{1,0:T(8,128)(2,1)S(1)}, u32[]{:S(2)}, u32[]{:S(2)}) collective-permute-start(bf16[512,128]{1,0:T(8,128)(2,1)} %bitcast.10), channel_id=1, source_target_pairs={{0,1},{1,0},{2,3},{3,2},{4,5},{5,4},{6,7},{7,6},{8,9},{9,8},{10,11... | collective-permute-start | bytes 393224 | tf_op jit(solution)/shard_map/ppermute | solution.py:297
  3.7 0.7 %copy-start.1 = (bf16[2,32,128]{2,1,0:T(8,128)(2,1)S(1)}, bf16[2,32,128]{2,1,0:T(8,128)(2,1)}, u32[]{:S(2)}) copy-start(bf16[2,32,128]{2,1,0:T(8,128)(2,1)} %queries_ref.1) | copy-start | bytes 49156
  5.1 6.5 %copy-start = (bf16[1,512,128]{2,1,0:T(8,128)(2,1)S(1)}, bf16[1,512,128]{2,1,0:T(8,128)(2,1)}, u32[]{:S(2)}) copy-start(bf16[1,512,128]{2,1,0:T(8,128)(2,1)} %param.5) | copy-start | bytes 393220
  5.1 10.9 %all-to-all-start = ((bf16[8,64,128]{2,1,0:T(8,128)(2,1)}), bf16[8,64,128]{2,1,0:T(8,128)(2,1)S(1)}, u32[]{:S(2)}, u32[]{:S(2)}) async-start(bf16[8,64,128]{2,1,0:T(8,128)(2,1)} %bitcast.1), calls=%async_computation | async-start | bytes 262144 | tf_op jit(solution)/shard_map/all_to_all | solution.py:291
  11.7 4.4 %collective-permute-start.2 = (bf16[512,128]{1,0:T(8,128)(2,1)S(1)}, bf16[512,128]{1,0:T(8,128)(2,1)S(1)}, u32[]{:S(2)}, u32[]{:S(2)}) collective-permute-start(bf16[512,128]{1,0:T(8,128)(2,1)S(1)} %bitcast.11), channel_id=1, source_target_pairs={{0,2},{2,0},{4,6},{6,4},{8,10},{10,8},{12,14},{14,12},{16,18},{18,... | collective-permute-start | bytes 393224 | tf_op jit(solution)/shard_map/ppermute | solution.py:298
  12.3 0.7 %copy-start.2 = (s32[32,1]{0,1:T(1,128)S(1)}, s32[32,1]{0,1:T(1,128)}, u32[]{:S(2)}) copy-start(s32[32,1]{0,1:T(1,128)} %param.7) | copy-start | bytes 388
  12.3 3.7 %collective-permute-start.3 = (bf16[512,128]{1,0:T(8,128)(2,1)S(1)}, bf16[512,128]{1,0:T(8,128)(2,1)S(1)}, u32[]{:S(2)}, u32[]{:S(2)}) collective-permute-start(bf16[512,128]{1,0:T(8,128)(2,1)S(1)} %collective-permute-done.1.far_ref), channel_id=1, source_target_pairs={{0,2},{2,0},{4,6},{6,4},{8,10},{10,8},{12,14},{14,12},{16,18},{18,... | collective-permute-start | bytes 393224 | tf_op jit(solution)/shard_map/ppermute | solution.py:299
  13.0 1.3 %collective-permute-start = (s32[33]{0:T(128)S(1)}, s32[33]{0:T(128)S(1)}, u32[]{:S(2)}, u32[]{:S(2)}) collective-permute-start(s32[33]{0:T(128)S(1)} %pad_add_fusion.facts_ref), channel_id=1, source_target_pairs={{0,2},{2,0},{4,6},{6,4},{8,10},{10,8},{12,14},{14,12},{16,18},{18,... | collective-permute-start | bytes 404 | tf_op jit(solution)/shard_map/ppermute | solution.py:301
  18.1 9.8 %all-to-all-start.1 = ((bf16[16,32,128]{2,1,0:T(8,128)(2,1)}), bf16[16,32,128]{2,1,0:T(8,128)(2,1)S(1)}, u32[]{:S(2)}, u32[]{:S(2)}) async-start(bf16[16,32,128]{2,1,0:T(8,128)(2,1)} %bitcast.5), calls=%async_computation.1 | async-start | bytes 262144 | tf_op jit(solution)/shard_map/all_to_all | solution.py:348
  24.7 1.4 %collective-permute-start.4 = (bf16[528,128]{1,0:T(8,128)(2,1)S(1)}, bf16[528,128]{1,0:T(8,128)(2,1)S(1)}, u32[]{:S(2)}, u32[]{:S(2)}) collective-permute-start(bf16[528,128]{1,0:T(8,128)(2,1)S(1)} %get-tuple-element.20), channel_id=1, source_target_pairs={{0,2},{2,0},{4,6},{6,4},{8,10},{10,8},{12,14},{14,12},{16,18},{18,... | collective-permute-start | bytes 405512 | tf_op jit(solution)/shard_map/ppermute | solution.py:366
